TPU v7x, 32 devices: a whole 2x2x4 slice. The times are simulated.
32 devices in a mesh: dp: 2 (over x), ctx: 4 (over y, core), tensor: 4 (over z).
Axes of the slice: x: 2, y: 2, z: 4, core: 2. Of those that a mesh axis runs over, the one named last changes fastest.
Arguments:
- tokens: bfloat16 [2, 4096, 768], P('dp', 'ctx'), may hold values from -6 to 6
- segment_ids: int32 [2, 4096], P('dp'), may hold values from 0 to 4, never falling along the last dimension, each value on 1 to 2000 neighbouring positions
- routes: int32 [2, 4096, 2], P('dp', 'ctx'), may hold values from 0 to 15, all different within a row
- pair_order: int32 [2, 4, 2048], P('dp', 'ctx'), may hold values from 0 to 2047, each once within a row
- gain_attn: bfloat16 [768], P(('dp', 'ctx')), may hold values from 0.099609375 to 1.8984375
- qkv_weight: bfloat16 [3, 768, 768], P(None, ('dp', 'ctx'), 'tensor'), may hold values from -0.21875 to 0.21875
- out_weight: bfloat16 [768, 768], P(('dp', 'ctx'), 'tensor'), may hold values from -2 to 2
- gain_ffn: bfloat16 [768], P(('dp', 'ctx')), may hold values from 0.099609375 to 1.8984375
- router_weight: bfloat16 [768, 16], P(('dp', 'ctx')), may hold values from -0.15625 to 0.15625
- shared_in: bfloat16 [2, 768, 2048], P(None, ('dp', 'ctx'), 'tensor'), may hold values from -0.21875 to 0.21875
- shared_out: bfloat16 [768, 2048], P(('dp', 'ctx'), 'tensor'), may hold values from -0.125 to 0.125
- expert_in: bfloat16 [16, 2, 768, 2048], P('dp', None, 'ctx', 'tensor'), may hold values from -0.21875 to 0.21875
- expert_out: bfloat16 [16, 768, 2048], P('dp', 'ctx', 'tensor'), may hold values from -0.125 to 0.125
- out_grad: bfloat16 [2, 4096, 768], P('dp', 'ctx'), may hold values from -6 to 6
Outputs:
- layer_out: bfloat16 [2, 4096, 768], P('dp', 'ctx')
- grad_tokens: float32 [2, 4096, 768], P('dp', 'ctx')
- grad_gain_attn: float32 [768], P(('dp', 'ctx'))
- grad_qkv: float32 [3, 768, 768], P(None, ('dp', 'ctx'), 'tensor')
- grad_out_weight: float32 [768, 768], P(('dp', 'ctx'), 'tensor')
- grad_gain_ffn: float32 [768], P(('dp', 'ctx'))
- grad_router: float32 [768, 16], P(('dp', 'ctx'))
- grad_shared_in: float32 [2, 768, 2048], P(None, ('dp', 'ctx'), 'tensor')
- grad_shared_out: float32 [768, 2048], P(('dp', 'ctx'), 'tensor')
- grad_expert_in: float32 [16, 2, 768, 2048], P('dp', None, 'ctx', 'tensor')
- grad_expert_out: float32 [16, 768, 2048], P('dp', 'ctx', 'tensor')
Inputs may be any that keep to these rules, and one draw needn't show every extreme that they name: `segment_ids`: along a sequence the document numbers never fall; a document spans at most 2000 consecutive tokens, and in every sequence one spans exactly that many. The two routes of a token name different experts. `pair_order`: for every sequence and routing group, a permutation of the numbers of its 2048 pairs.
All inputs are finite; a program needn't handle non-finite values.
Results may differ from a plain program's by a relative error of at most 0.015.
Values may be sent and summed in bfloat16 or wider, within the bound.
No kernel may reach another device: no remote copies, remote signals or barrier semaphores. Data moves between devices by JAX's collectives and lax.ppermute only.
A program may use at most 256 MiB of HBM per device.

v0:
```python
import math

import jax
import jax.numpy as jnp
from jax import lax
from jax.sharding import PartitionSpec as P

HD = 64


EPSILON = 1e-06


def rms_norm(values, norm_gain):
    return (
        values * lax.rsqrt(jnp.mean(values * values, axis=-1, keepdims=True) + EPSILON) * norm_gain
    )


def rope_tables(positions, head_size):
    half_size = head_size // 2
    inverse = 1.0 / 10000.0 ** (jnp.arange(half_size, dtype=jnp.float32) * (2.0 / head_size))
    angles = positions.astype(jnp.float32)[:, None] * inverse[None, :]
    return (jnp.cos(angles)[:, None, :], jnp.sin(angles)[:, None, :])


def rotate(values, cos_table, sin_table):
    half_size = values.shape[-1] // 2
    first_half = values[..., :half_size]
    second_half = values[..., half_size:]
    return jnp.concatenate(
        [
            first_half * cos_table - second_half * sin_table,
            second_half * cos_table + first_half * sin_table,
        ],
        axis=-1,
    )


def unrotate(grad_values, cos_table, sin_table):
    half_size = grad_values.shape[-1] // 2
    first_half = grad_values[..., :half_size]
    second_half = grad_values[..., half_size:]
    return jnp.concatenate(
        [
            first_half * cos_table + second_half * sin_table,
            second_half * cos_table - first_half * sin_table,
        ],
        axis=-1,
    )


def swiglu(gate_pre, up_pre):
    return jax.nn.silu(gate_pre) * up_pre


def slot_tables(group_routes, group_order, experts, capacity):
    pair_count = group_order.shape[0]
    pair_expert = group_routes.reshape(pair_count)
    ranked = pair_expert[group_order]
    onehot = (ranked[:, None] == jnp.arange(experts, dtype=jnp.int32)[None, :]).astype(jnp.int32)
    earlier = jnp.cumsum(onehot, axis=0, dtype=jnp.int32) - onehot
    ranked_slot = jnp.sum(earlier * onehot, axis=1, dtype=jnp.int32)
    slot_index = jnp.zeros((pair_count,), jnp.int32).at[group_order].set(ranked_slot)
    pair_place = jnp.where(
        slot_index < capacity, pair_expert * capacity + slot_index, experts * capacity
    )
    slot_pair = (
        jnp.full((experts * capacity,), pair_count, jnp.int32)
        .at[pair_place]
        .set(jnp.arange(pair_count, dtype=jnp.int32), mode="drop")
    )
    return (pair_place, slot_pair)


def score_block(query_block, key_head, block_pos, block_seg, seg_all, score_scale):
    raw_scores = (
        jnp.einsum("qd,kd->qk", query_block, key_head, preferred_element_type=jnp.float32)
        * score_scale
    )
    key_pos = jnp.arange(key_head.shape[0], dtype=jnp.int32)
    allowed = (key_pos[None, :] <= block_pos[:, None]) & (seg_all[None, :] == block_seg[:, None])
    return jnp.where(allowed, raw_scores, -1e30)


def head_forward(query_head, key_head, value_head, pos_blocks, seg_blocks, seg_all, score_scale):

    def one_block(block_inputs):
        query_block, block_pos, block_seg = block_inputs
        scores = score_block(query_block, key_head, block_pos, block_seg, seg_all, score_scale)
        row_peak = jnp.max(scores, axis=1, keepdims=True)
        exponent = jnp.exp(scores - row_peak)
        row_total = jnp.sum(exponent, axis=1, keepdims=True)
        attn_probs = (exponent / row_total).astype(jnp.bfloat16)
        attended = jnp.dot(attn_probs, value_head, preferred_element_type=jnp.float32)
        return (attended.astype(jnp.bfloat16), row_peak[:, 0] + jnp.log(row_total[:, 0]))

    return lax.map(one_block, (query_head, pos_blocks, seg_blocks))


def head_backward(
    query_head,
    key_head,
    value_head,
    dout_head,
    log_total,
    pos_blocks,
    seg_blocks,
    seg_all,
    score_scale,
):

    def one_block(carry, block_inputs):
        key_grad, value_grad = carry
        query_block, dout_block, block_lse, block_pos, block_seg = block_inputs
        scores = score_block(query_block, key_head, block_pos, block_seg, seg_all, score_scale)
        probs_full = jnp.exp(scores - block_lse[:, None])
        dprobs = jnp.einsum("qd,kd->qk", dout_block, value_head, preferred_element_type=jnp.float32)
        delta_rows = jnp.sum(probs_full * dprobs, axis=1, keepdims=True)
        dscores = (probs_full * (dprobs - delta_rows)).astype(jnp.bfloat16)
        query_grad = jnp.dot(dscores, key_head, preferred_element_type=jnp.float32) * score_scale
        key_grad = (
            key_grad
            + jnp.einsum("qk,qd->kd", dscores, query_block, preferred_element_type=jnp.float32)
            * score_scale
        )
        value_grad = value_grad + jnp.einsum(
            "qk,qd->kd",
            probs_full.astype(jnp.bfloat16),
            dout_block,
            preferred_element_type=jnp.float32,
        )
        return ((key_grad, value_grad), query_grad)

    zero_rows = jnp.zeros(key_head.shape, jnp.float32)
    (key_grad, value_grad), query_grad = lax.scan(
        one_block,
        (zero_rows, zero_rows),
        (query_head, dout_head, log_total, pos_blocks, seg_blocks),
    )
    return (query_grad, key_grad, value_grad)


def expert_pre(rows_in, weights_in):
    gate_pre = jnp.einsum(
        "erd,edf->erf", rows_in, weights_in[:, 0], preferred_element_type=jnp.float32
    )
    up_pre = jnp.einsum(
        "erd,edf->erf", rows_in, weights_in[:, 1], preferred_element_type=jnp.float32
    )
    return (gate_pre, up_pre)


def shared_pre(rows_in, weights_in):
    gate_pre = jnp.dot(rows_in, weights_in[0], preferred_element_type=jnp.float32)
    up_pre = jnp.dot(rows_in, weights_in[1], preferred_element_type=jnp.float32)
    return (gate_pre, up_pre)


def shards(
    tokens,
    segment_ids,
    routes,
    pair_order,
    gain_attn,
    qkv_weight,
    out_weight,
    gain_ffn,
    router_weight,
    shared_in,
    shared_out,
    expert_in,
    expert_out,
    out_grad,
):
    row_count = tokens.shape[1]
    inputs = tokens[0].astype(jnp.float32)
    grad_layer = out_grad[0].astype(jnp.float32)
    seg_all = segment_ids[0]
    my_routes = routes[0]
    my_order = pair_order[0, 0]
    qkv_full, out_full, shin_full, shout_full, router_full, attn_gain, ffn_gain = (
        lax.all_gather(qkv_weight, ("dp", "ctx"), axis=1, tiled=True),
        lax.all_gather(out_weight, ("dp", "ctx"), axis=0, tiled=True),
        lax.all_gather(shared_in, ("dp", "ctx"), axis=1, tiled=True),
        lax.all_gather(shared_out, ("dp", "ctx"), axis=0, tiled=True),
        lax.all_gather(router_weight, ("dp", "ctx"), axis=0, tiled=True),
        lax.all_gather(gain_attn, ("dp", "ctx"), axis=0, tiled=True),
        lax.all_gather(gain_ffn, ("dp", "ctx"), axis=0, tiled=True),
    )
    attn_gain = attn_gain.astype(jnp.float32)
    ffn_gain = ffn_gain.astype(jnp.float32)
    expert_count = router_full.shape[1]
    capacity = 10 * row_count // (4 * expert_count)
    score_scale = 1.0 / math.sqrt(HD)
    normed = rms_norm(inputs, attn_gain).astype(jnp.bfloat16)
    q_raw = jnp.dot(normed, qkv_full[0], preferred_element_type=jnp.float32)
    k_raw = jnp.dot(normed, qkv_full[1], preferred_element_type=jnp.float32)
    v_raw = jnp.dot(normed, qkv_full[2], preferred_element_type=jnp.float32)
    head_count = q_raw.shape[1] // HD
    row_start = lax.axis_index("ctx") * row_count
    query_pos = row_start + jnp.arange(row_count, dtype=jnp.int32)
    query_seg = lax.dynamic_slice_in_dim(seg_all, row_start, row_count)
    cos_table, sin_table = rope_tables(query_pos, HD)
    query_rot = rotate(q_raw.reshape(row_count, head_count, HD), cos_table, sin_table).astype(
        jnp.bfloat16
    )
    key_local = (
        rotate(k_raw.reshape(row_count, head_count, HD), cos_table, sin_table)
        .astype(jnp.bfloat16)
        .reshape(row_count, head_count * HD)
    )
    value_local = v_raw.astype(jnp.bfloat16)
    key_all, value_all, ein_full, eout_full = (
        lax.all_gather(key_local, "ctx", axis=0, tiled=True),
        lax.all_gather(value_local, "ctx", axis=0, tiled=True),
        lax.all_gather(expert_in, "ctx", axis=2, tiled=True),
        lax.all_gather(expert_out, "ctx", axis=1, tiled=True),
    )
    block_rows = 512
    block_count = row_count // block_rows
    pos_blocks = query_pos.reshape(block_count, block_rows)
    seg_blocks = query_seg.reshape(block_count, block_rows)
    full_len = key_all.shape[0]
    key_heads = key_all.reshape(full_len, head_count, HD)
    value_heads = value_all.reshape(full_len, head_count, HD)
    attended_list = []
    lse_list = []
    for head_index in range(head_count):
        head_out, head_lse = head_forward(
            query_rot[:, head_index, :].reshape(block_count, block_rows, HD),
            key_heads[:, head_index, :],
            value_heads[:, head_index, :],
            pos_blocks,
            seg_blocks,
            seg_all,
            score_scale,
        )
        attended_list.append(head_out.reshape(row_count, HD))
        lse_list.append(head_lse)
    attended = jnp.concatenate(attended_list, axis=1)
    branch_part = jnp.einsum("lc,dc->ld", attended, out_full, preferred_element_type=jnp.float32)
    branch = lax.psum(branch_part, "tensor")
    residual = inputs + branch
    normed2 = rms_norm(residual, ffn_gain).astype(jnp.bfloat16)
    logits = jnp.dot(normed2, router_full, preferred_element_type=jnp.float32)
    expert_ids = jnp.arange(expert_count, dtype=jnp.int32)
    picked = my_routes[:, :, None] == expert_ids[None, None, :]
    chosen = jnp.sum(jnp.where(picked, logits[:, None, :], 0.0), axis=2)
    chosen_peak = jnp.max(chosen, axis=1, keepdims=True)
    chosen_exp = jnp.exp(chosen - chosen_peak)
    gate_probs = chosen_exp / jnp.sum(chosen_exp, axis=1, keepdims=True)
    pair_place, slot_pair = slot_tables(my_routes, my_order, expert_count, capacity)
    slot_token = slot_pair // 2
    send_width = normed2.shape[1]
    padded = jnp.concatenate([normed2, jnp.zeros((1, send_width), jnp.bfloat16)], axis=0)
    send_rows = padded[slot_token].reshape(expert_count, capacity, send_width)
    gate_flat = jnp.concatenate(
        [gate_probs.reshape(2 * row_count), jnp.zeros((1,), jnp.float32)], axis=0
    )
    grad_pad = jnp.concatenate([grad_layer, jnp.zeros((1, send_width), jnp.float32)], axis=0)
    slot_grad = (
        (gate_flat[slot_pair][:, None] * grad_pad[slot_token])
        .astype(jnp.bfloat16)
        .reshape(expert_count, capacity, send_width)
    )
    received, grad_rows = (
        lax.all_to_all(send_rows, "dp", split_axis=0, concat_axis=1, tiled=True),
        lax.all_to_all(slot_grad, "dp", split_axis=0, concat_axis=1, tiled=True),
    )
    gate_pre, up_pre = expert_pre(received, ein_full)
    hidden = swiglu(gate_pre, up_pre).astype(jnp.bfloat16)
    expert_part = jnp.einsum("erf,edf->erd", hidden, eout_full, preferred_element_type=jnp.float32)
    returned = lax.all_to_all(expert_part, "dp", split_axis=1, concat_axis=0, tiled=True)
    flat_rows = jnp.concatenate(
        [
            returned.reshape(expert_count * capacity, send_width),
            jnp.zeros((1, send_width), jnp.float32),
        ],
        axis=0,
    )
    paired = flat_rows[pair_place].reshape(row_count, 2, send_width)
    combined = jnp.sum(gate_probs[:, :, None] * paired, axis=1)
    s_gate, s_up = shared_pre(normed2, shin_full)
    shared_hidden = swiglu(s_gate, s_up).astype(jnp.bfloat16)
    shared_part = jnp.einsum(
        "lf,df->ld", shared_hidden, shout_full, preferred_element_type=jnp.float32
    )
    ffn_total = lax.psum((combined + shared_part).astype(jnp.bfloat16), "tensor").astype(
        jnp.float32
    )
    layer_out = (residual + ffn_total).astype(jnp.bfloat16)
    normed_again, received_again = lax.optimization_barrier((normed2, received))
    s_gate_back, s_up_back = shared_pre(normed_again, shin_full)
    gate_back, up_back = expert_pre(received_again, ein_full)
    grad_low = out_grad[0]
    shared_value, shared_pull = jax.vjp(swiglu, s_gate_back, s_up_back)
    shared_hid_back = shared_value.astype(jnp.bfloat16)
    shared_dh = jnp.einsum("ld,df->lf", grad_low, shout_full, preferred_element_type=jnp.float32)
    ds_gate, ds_up = shared_pull(shared_dh)
    ds_gate = ds_gate.astype(jnp.bfloat16)
    ds_up = ds_up.astype(jnp.bfloat16)
    grad_shout = jnp.einsum(
        "ld,lf->df", grad_low, shared_hid_back, preferred_element_type=jnp.float32
    )
    grad_shin = jnp.stack(
        [
            jnp.einsum("ld,lf->df", normed2, ds_gate, preferred_element_type=jnp.float32),
            jnp.einsum("ld,lf->df", normed2, ds_up, preferred_element_type=jnp.float32),
        ],
        axis=0,
    )
    dnormed2 = jnp.einsum(
        "lf,df->ld", ds_gate, shin_full[0], preferred_element_type=jnp.float32
    ) + jnp.einsum("lf,df->ld", ds_up, shin_full[1], preferred_element_type=jnp.float32)
    expert_value, expert_pull = jax.vjp(swiglu, gate_back, up_back)
    hidden_back = expert_value.astype(jnp.bfloat16)
    dhidden = jnp.einsum("erd,edf->erf", grad_rows, eout_full, preferred_element_type=jnp.float32)
    dgate_pre, dup_pre = expert_pull(dhidden)
    dgate_pre = dgate_pre.astype(jnp.bfloat16)
    dup_pre = dup_pre.astype(jnp.bfloat16)
    grad_eout = jnp.einsum(
        "erd,erf->edf", grad_rows, hidden_back, preferred_element_type=jnp.float32
    )
    grad_ein = jnp.stack(
        [
            jnp.einsum("erd,erf->edf", received, dgate_pre, preferred_element_type=jnp.float32),
            jnp.einsum("erd,erf->edf", received, dup_pre, preferred_element_type=jnp.float32),
        ],
        axis=1,
    )
    row_grads = jnp.einsum(
        "erf,edf->erd", dgate_pre, ein_full[:, 0], preferred_element_type=jnp.float32
    ) + jnp.einsum("erf,edf->erd", dup_pre, ein_full[:, 1], preferred_element_type=jnp.float32)
    grad_back = lax.all_to_all(row_grads, "dp", split_axis=1, concat_axis=0, tiled=True)
    back_flat = jnp.concatenate(
        [
            grad_back.reshape(expert_count * capacity, send_width),
            jnp.zeros((1, send_width), jnp.float32),
        ],
        axis=0,
    )
    back_sum = jnp.sum(back_flat[pair_place].reshape(row_count, 2, send_width), axis=1)
    dnormed2 = dnormed2 + back_sum
    dgates = jnp.sum(paired * grad_layer[:, None, :], axis=2)
    dnormed2, dgates = lax.psum((dnormed2, dgates), "tensor")
    dchosen = gate_probs * (dgates - jnp.sum(gate_probs * dgates, axis=1, keepdims=True))
    dlogits = jnp.sum(jnp.where(picked, dchosen[:, :, None], 0.0), axis=1).astype(jnp.bfloat16)
    grad_router = jnp.einsum("ld,le->de", normed2, dlogits, preferred_element_type=jnp.float32)
    dnormed2 = dnormed2 + jnp.einsum(
        "le,de->ld", dlogits, router_full, preferred_element_type=jnp.float32
    )
    norm2_pull = jax.vjp(rms_norm, residual, ffn_gain)[1]
    dresid_norm, grad_gain2 = norm2_pull(dnormed2)
    dresid = grad_layer + dresid_norm
    dbranch = dresid.astype(jnp.bfloat16)
    grad_outw = jnp.einsum("ld,lc->dc", dbranch, attended, preferred_element_type=jnp.float32)
    dattended = jnp.einsum(
        "ld,dc->lc", dbranch, out_full, preferred_element_type=jnp.float32
    ).astype(jnp.bfloat16)
    dq_list = []
    dk_list = []
    dv_list = []
    for head_index in range(head_count):
        dout_head = dattended[:, head_index * HD : (head_index + 1) * HD].reshape(
            block_count, block_rows, HD
        )
        query_grad, key_grad, value_grad = head_backward(
            query_rot[:, head_index, :].reshape(block_count, block_rows, HD),
            key_heads[:, head_index, :],
            value_heads[:, head_index, :],
            dout_head,
            lse_list[head_index],
            pos_blocks,
            seg_blocks,
            seg_all,
            score_scale,
        )
        dq_list.append(query_grad.reshape(row_count, HD))
        dk_list.append(key_grad)
        dv_list.append(value_grad)
    dquery = jnp.stack(dq_list, axis=1)
    dkey_all = jnp.concatenate(dk_list, axis=1)
    dvalue_all = jnp.concatenate(dv_list, axis=1)
    dkey_mine, dvalue_mine, grad_ein_mine, grad_eout_mine = (
        lax.psum_scatter(dkey_all, "ctx", scatter_dimension=0, tiled=True),
        lax.psum_scatter(dvalue_all, "ctx", scatter_dimension=0, tiled=True),
        lax.psum_scatter(grad_ein, "ctx", scatter_dimension=2, tiled=True),
        lax.psum_scatter(grad_eout, "ctx", scatter_dimension=1, tiled=True),
    )
    dq_raw = (
        unrotate(dquery, cos_table, sin_table)
        .reshape(row_count, head_count * HD)
        .astype(jnp.bfloat16)
    )
    dk_raw = (
        unrotate(dkey_mine.reshape(row_count, head_count, HD), cos_table, sin_table)
        .reshape(row_count, head_count * HD)
        .astype(jnp.bfloat16)
    )
    dv_raw = dvalue_mine.astype(jnp.bfloat16)
    grad_qkv = jnp.stack(
        [
            jnp.einsum("ld,lc->dc", normed, dq_raw, preferred_element_type=jnp.float32),
            jnp.einsum("ld,lc->dc", normed, dk_raw, preferred_element_type=jnp.float32),
            jnp.einsum("ld,lc->dc", normed, dv_raw, preferred_element_type=jnp.float32),
        ],
        axis=0,
    )
    dnormed = (
        jnp.einsum("lc,dc->ld", dq_raw, qkv_full[0], preferred_element_type=jnp.float32)
        + jnp.einsum("lc,dc->ld", dk_raw, qkv_full[1], preferred_element_type=jnp.float32)
        + jnp.einsum("lc,dc->ld", dv_raw, qkv_full[2], preferred_element_type=jnp.float32)
    )
    dnormed = lax.psum(dnormed, "tensor")
    norm1_pull = jax.vjp(rms_norm, inputs, attn_gain)[1]
    dinputs_norm, grad_gain1 = norm1_pull(dnormed)
    grad_tokens = dresid + dinputs_norm
    total_qkv, total_outw, total_shin, total_shout, total_router, total_gain1, total_gain2 = (
        lax.psum_scatter(grad_qkv, ("dp", "ctx"), scatter_dimension=1, tiled=True),
        lax.psum_scatter(grad_outw, ("dp", "ctx"), scatter_dimension=0, tiled=True),
        lax.psum_scatter(grad_shin, ("dp", "ctx"), scatter_dimension=1, tiled=True),
        lax.psum_scatter(grad_shout, ("dp", "ctx"), scatter_dimension=0, tiled=True),
        lax.psum_scatter(grad_router, ("dp", "ctx"), scatter_dimension=0, tiled=True),
        lax.psum_scatter(grad_gain1, ("dp", "ctx"), scatter_dimension=0, tiled=True),
        lax.psum_scatter(grad_gain2, ("dp", "ctx"), scatter_dimension=0, tiled=True),
    )
    return (
        layer_out[None],
        grad_tokens[None],
        total_gain1,
        total_qkv,
        total_outw,
        total_gain2,
        total_router,
        total_shin,
        total_shout,
        grad_ein_mine,
        grad_eout_mine,
    )


def solution(mesh):
    return jax.shard_map(
        shards,
        mesh=mesh,
        in_specs=(
            P("dp", "ctx", None),
            P("dp", None),
            P("dp", "ctx", None),
            P("dp", "ctx", None),
            P(("dp", "ctx")),
            P(None, ("dp", "ctx"), "tensor"),
            P(("dp", "ctx"), "tensor"),
            P(("dp", "ctx")),
            P(("dp", "ctx"), None),
            P(None, ("dp", "ctx"), "tensor"),
            P(("dp", "ctx"), "tensor"),
            P("dp", None, "ctx", "tensor"),
            P("dp", "ctx", "tensor"),
            P("dp", "ctx", None),
        ),
        out_specs=(
            P("dp", "ctx", None),
            P("dp", "ctx", None),
            P(("dp", "ctx")),
            P(None, ("dp", "ctx"), "tensor"),
            P(("dp", "ctx"), "tensor"),
            P(("dp", "ctx")),
            P(("dp", "ctx"), None),
            P(None, ("dp", "ctx"), "tensor"),
            P(("dp", "ctx"), "tensor"),
            P("dp", None, "ctx", "tensor"),
            P("dp", "ctx", "tensor"),
        ),
        check_vma=False,
    )
```

profile of v0, /device:TPU:0, one launch (start us, length us, event | category | flops | bytes accessed | tf_op | source)
XLA Modules:
  0.0 1818.1 jit_solution(1218304723929365828)
XLA Ops:
  8.1 13.4 all_gather.34
  24.3 13.8 all-reduce.9
  47.7 12.1 all_gather.37
  67.3 19.1 %all-gather.9.cloned.1.call-done = bf16[4096,192]{0,1:T(8,128)(2,1)} async-done(((bf16[1024,192]{0,1:T(8,128)(2,1)}), bf16[4096,192]{0,1:T(8,128)(2,1)}) %all-gather.9.cloned.1.call-update) | async-done | bytes 1572880 | tf_op jit(solution)/shard_map/all_gather | solution.py:216
  90.5 12.1 while.81
  106.1 13.3 while.82
  124.9 15.9 while.83
  186.5 82.1 %all-reduce.15.cloned.1.call-done = f32[1024,768]{1,0:T(8,128)} async-done(((f32[1024,768]{1,0:T(8,128)}), f32[1024,768]{1,0:T(8,128)}) %all-reduce.15.cloned.1.call-update) | async-done | bytes 3145744 | tf_op jit(solution)/shard_map/psum | solution.py:243
  298.5 37.0 %all-gather = bf16[8,96,16]{1,2,0:T(8,128)(2,1)S(1)} all-gather(bf16[1,96,16]{1,2,0:T(8,128)(2,1)S(1)} %bitcast.565), channel_id=1, replica_groups=mesh['dp'=2,'ctx'=4,'tensor'=4] {'dp','ctx'}, dimensions={0}, use_global_device_ids=true | all-gather | bytes 27648 | tf_op jit(solution)/shard_map/all_gather | solution.py:187
  340.1 13.6 gather_fusion.3
  369.7 41.1 %all-to-all-done.2 = bf16[16,160,768]{2,1,0:T(8,128)(2,1)} async-done(((bf16[16,160,768]{2,1,0:T(8,128)(2,1)}), bf16[16,160,768]{2,1,0:T(8,128)(2,1)}, u32[]{:S(2)}, u32[]{:S(2)}) %all-to-all-start.2) | async-done | bytes 3932192 | tf_op jit(solution)/shard_map/all_to_all | solution.py:269
  478.1 14.7 fusion.105
  503.7 58.2 %all-to-all-done.3 = f32[8,320,768]{2,0,1:T(8,128)} async-done(((f32[8,320,768]{2,0,1:T(8,128)}), f32[8,320,768]{2,0,1:T(8,128)}, u32[]{:S(2)}, u32[]{:S(2)}) %all-to-all-start.3) | async-done | bytes 7864352 | tf_op jit(solution)/shard_map/all_to_all | solution.py:335
  568.7 92.8 %all_gather.43 = bf16[768,512]{1,0:T(8,128)(2,1)} all-gather(bf16[96,512]{1,0:T(8,128)(2,1)S(1)} %copy-done.80), channel_id=1, replica_groups=mesh['dp'=2,'ctx'=4,'tensor'=4] {'dp','ctx'}, dimensions={0}, use_global_device_ids=true | all-gather | bytes 884736 | tf_op jit(solution)/shard_map/all_gather | solution.py:186
  680.8 13.9 gather_fusion.5
  733.0 13.9 gather_fusion.2
  755.2 17.2 multiply_reduce_fusion.3
  791.2 49.7 %all-reduce.19.cloned.1.call-done = f32[1024,768]{1,0:T(8,128)} async-done(((f32[1024,768]{1,0:T(8,128)}), f32[1024,768]{1,0:T(8,128)}) %all-reduce.19.cloned.1.call-update) | async-done | bytes 3145744 | tf_op jit(solution)/shard_map/psum | solution.py:346
  847.1 64.7 %all-reduce.17.cloned.1.call-done = bf16[1024,768]{1,0:T(8,128)(2,1)} async-done(((bf16[1024,768]{1,0:T(8,128)(2,1)}), bf16[1024,768]{1,0:T(8,128)(2,1)}) %all-reduce.17.cloned.1.call-update) | async-done | bytes 1572880 | tf_op jit(solution)/shard_map/psum | solution.py:289
  921.0 63.0 %while.86 = (s32[]{:T(128)}, f32[4096,64]{0,1:T(8,128)S(1)}, f32[4096,64]{0,1:T(8,128)S(1)}, f32[2,512,64]{1,0,2:T(2,128)}, s32[2,512]{1,0:T(2,128)S(1)}, /*inde...) while((s32[]{:T(128)}, f32[4096,64]{0,1:T(8,128)S(1)}, ...), condition=%wide.region_40.41_spmd.clone, body=%wide.region_38.40_spmd.clone.sunk | while | flops 1368686080 | bytes 125540712 | solution.py:136
  986.0 65.3 %while.85 = (s32[]{:T(128)}, f32[4096,64]{0,1:T(8,128)}, f32[4096,64]{0,1:T(8,128)S(1)}, f32[2,512,64]{1,0,2:T(2,128)}, s32[2,512]{1,0:T(2,128)S(1)}, /*index=5*...) while((s32[]{:T(128)}, f32[4096,64]{0,1:T(8,128)}, ...), condition=%wide.region_37.38_spmd.clone, body=%wide.region_35.37_spmd.clone.sunk | while | flops 1368686080 | bytes 125540712 | solution.py:136
  1053.1 63.1 %while.84 = (s32[]{:T(128)}, f32[4096,64]{0,1:T(8,128)S(1)}, f32[4096,64]{0,1:T(8,128)S(1)}, f32[2,512,64]{1,0,2:T(2,128)}, s32[2,512]{1,0:T(2,128)S(1)}, /*inde...) while((s32[]{:T(128)}, f32[4096,64]{0,1:T(8,128)S(1)}, ...), condition=%wide.region_34.35_spmd.clone, body=%wide.region_32.34_spmd.clone.sunk | while | flops 1368686080 | bytes 125540712 | solution.py:136
  1126.9 29.9 %reduce-scatter.16.cloned.1.call-done = f32[1024,192]{0,1:T(8,128)} async-done(((f32[4096,192]{0,1:T(8,128)}), f32[1024,192]{0,1:T(8,128)}) %reduce-scatter.16.cloned.1.call-update) | async-done | bytes 786448 | tf_op jit(solution)/shard_map/reduce_scatter | solution.py:386
  1159.6 38.1 %reduce-scatter.18.cloned.1.call-done = f32[1024,192]{0,1:T(8,128)} async-done(((f32[4096,192]{0,1:T(8,128)}), f32[1024,192]{0,1:T(8,128)}) %reduce-scatter.18.cloned.1.call-update) | async-done | bytes 786448 | tf_op jit(solution)/shard_map/reduce_scatter | solution.py:387
  1252.4 13.3 fusion.106
  1280.6 122.0 %all-reduce.21.cloned.1.call-done = f32[1024,768]{1,0:T(8,128)} async-done(((f32[1024,768]{1,0:T(8,128)}), f32[1024,768]{1,0:T(8,128)}) %all-reduce.21.cloned.1.call-update) | async-done | bytes 3145744 | tf_op jit(solution)/shard_map/psum | solution.py:415
  1406.0 13.7 all-reduce.8
  1428.2 151.7 %reduce-scatter.24.cloned.1.call-done = f32[8,2,192,512]{3,2,0,1:T(8,128)} async-done(((f32[8,2,768,512]{3,2,0,1:T(8,128)}), f32[8,2,192,512]{3,2,0,1:T(8,128)}) %reduce-scatter.24.cloned.1.call-update) | async-done | bytes 6291472 | tf_op jit(solution)/shard_map/reduce_scatter | solution.py:388
  1586.4 35.6 %reduce-scatter.32.cloned.1.call-done = f32[96,512]{1,0:T(8,128)} async-done(((f32[768,512]{1,0:T(8,128)}), f32[96,512]{1,0:T(8,128)}) %reduce-scatter.32.cloned.1.call-update) | async-done | bytes 196624
  1622.0 49.9 %reduce-scatter.22.cloned.1.call-done = f32[2,96,512]{2,1,0:T(8,128)} async-done(((f32[2,768,512]{2,1,0:T(8,128)}), f32[2,96,512]{2,1,0:T(8,128)}) %reduce-scatter.22.cloned.1.call-update) | async-done | bytes 393232 | tf_op jit(solution)/shard_map/reduce_scatter | solution.py:422
  1671.9 38.5 %reduce-scatter.20.cloned.1.call-done = f32[96,192]{1,0:T(8,128)} async-done(((f32[768,192]{1,0:T(8,128)}), f32[96,192]{1,0:T(8,128)}) %reduce-scatter.20.cloned.1.call-update) | async-done | bytes 73744 | tf_op jit(solution)/shard_map/reduce_scatter | solution.py:421
  1710.4 100.3 %reduce-scatter.26.cloned.1.call-done = f32[8,192,512]{2,1,0:T(8,128)} async-done(((f32[8,768,512]{2,1,0:T(8,128)}), f32[8,192,512]{2,1,0:T(8,128)}) %reduce-scatter.26.cloned.1.call-update) | async-done | bytes 3145744 | tf_op jit(solution)/shard_map/reduce_scatter | solution.py:389
  (591 shorter events, 647.4 us)
Async XLA Ops:
  8.1 56.5 %all-gather.7.cloned.1.call-start = ((), (), s32[]{:S(2)}) async-start(), calls=%async_computation.13 | async-start | bytes 1966080 | tf_op jit(solution)/shard_map/all_gather | solution.py:215
  44.0 42.4 %all-gather.9.cloned.1.call-start = ((), (), s32[]{:S(2)}) async-start(), calls=%async_computation.14 | async-start | bytes 1966080 | tf_op jit(solution)/shard_map/all_gather | solution.py:216
  45.6 223.0 %all-reduce.15.cloned.1.call-start = ((), (), s32[]{:S(2)}) async-start(), calls=%async_computation.15 | async-start | bytes 6291456 | tf_op jit(solution)/shard_map/psum | solution.py:243
  147.4 267.7 %all-gather.11.cloned.1.call-start = ((), (), s32[]{:S(2)}) async-start(), calls=%async_computation.16 | async-start | bytes 15728640 | tf_op jit(solution)/shard_map/all_gather | solution.py:217
  151.4 278.9 %all-gather.13.cloned.1.call-start = ((), (), s32[]{:S(2)}) async-start(), calls=%async_computation.17 | async-start | bytes 7864320 | tf_op jit(solution)/shard_map/all_gather | solution.py:218
  152.0 119.0 %copy-start.84 = (f32[768]{0:T(1024)}, f32[768]{0:T(1024)S(1)}, u32[]{:S(2)}) copy-start(f32[768]{0:T(1024)S(1)} %convert_element_type.186) | copy-start | bytes 9220
  152.6 116.0 %copy-start.34 = (bf16[1,1024,768]{2,1,0:T(8,128)(2,1)S(1)}, bf16[1,1024,768]{2,1,0:T(8,128)(2,1)}, u32[]{:S(2)}) copy-start(bf16[1,1024,768]{2,1,0:T(8,128)(2,1)} %param.26) | copy-start | bytes 4718596
  281.9 77.7 %all-to-all-start = ((bf16[16,160,768]{2,1,0:T(8,128)(2,1)}), bf16[16,160,768]{2,1,0:T(8,128)(2,1)}, u32[]{:S(2)}, u32[]{:S(2)}) async-start(bf16[16,160,768]{2,1,0:T(8,128)(2,1)} %bitcast.513), calls=%async_computation | async-start | bytes 7864320 | tf_op jit(solution)/shard_map/all_to_all | solution.py:268
  359.5 51.2 %all-to-all-start.2 = ((bf16[16,160,768]{2,1,0:T(8,128)(2,1)}), bf16[16,160,768]{2,1,0:T(8,128)(2,1)}, u32[]{:S(2)}, u32[]{:S(2)}) async-start(bf16[16,160,768]{2,1,0:T(8,128)(2,1)} %multiply_convert_fusion.3), calls=%async_computation.2 | async-start | bytes 7864320 | tf_op jit(solution)/shard_map/all_to_all | solution.py:269
  462.1 99.8 %all-to-all-start.3 = ((f32[8,320,768]{2,0,1:T(8,128)}), f32[8,320,768]{2,0,1:T(8,128)}, u32[]{:S(2)}, u32[]{:S(2)}) async-start(f32[8,320,768]{2,0,1:T(8,128)} %copy.191), calls=%async_computation.3 | async-start | bytes 15728640 | tf_op jit(solution)/shard_map/all_to_all | solution.py:335
  468.9 192.6 %all-gather.15.cloned.1.call-start = ((), (), s32[]{:S(2)}) async-start(), calls=%async_computation.18 | async-start | bytes 1769472 | tf_op jit(solution)/shard_map/all_gather | solution.py:185
  503.7 157.9 %copy-start.30 = (bf16[1024,768]{1,0:T(8,128)(2,1)S(1)}, bf16[1024,768]{1,0:T(8,128)(2,1)}, u32[]{:S(2)}) copy-start(bf16[1024,768]{1,0:T(8,128)(2,1)} %copy-done.29) | copy-start | bytes 4718596
  561.9 161.4 %all-to-all-start.1 = ((f32[8,320,768]{2,0,1:T(8,128)}), f32[8,320,768]{2,0,1:T(8,128)}, u32[]{:S(2)}, u32[]{:S(2)}) async-start(f32[8,320,768]{2,0,1:T(8,128)} %copy.187), calls=%async_computation.1 | async-start | bytes 15728640 | tf_op jit(solution)/shard_map/all_to_all | solution.py:274
  568.7 272.2 %all-reduce.19.cloned.1.call-start = ((), (), s32[]{:S(2)}) async-start(), calls=%async_computation.20 | async-start | bytes 6291456 | tf_op jit(solution)/shard_map/psum | solution.py:346
  720.6 191.1 %all-reduce.17.cloned.1.call-start = ((), (), s32[]{:S(2)}) async-start(), calls=%async_computation.19 | async-start | bytes 3145728 | tf_op jit(solution)/shard_map/psum | solution.py:289
  772.4 68.5 %copy-start.77 = (bf16[768,16]{0,1:T(8,128)(2,1)S(1)}, bf16[768,16]{0,1:T(8,128)(2,1)}, u32[]{:S(2)}) copy-start(bf16[768,16]{0,1:T(8,128)(2,1)} %copy-done.76) | copy-start | bytes 73732
  772.4 68.5 %copy-start.85 = (f32[768]{0:T(1024)S(1)}, f32[768]{0:T(1024)}, u32[]{:S(2)}) copy-start(f32[768]{0:T(1024)} %copy-done.84) | copy-start | bytes 9220
  772.4 68.5 %copy-start.87 = (f32[1024]{0:T(1024)S(1)}, f32[1024]{0:T(1024)}, u32[]{:S(2)}) copy-start(f32[1024]{0:T(1024)} %copy-done.86) | copy-start | bytes 12292
  779.0 377.8 %reduce-scatter.16.cloned.1.call-start = ((), (), s32[]{:S(2)}) async-start(), calls=%async_computation.21 | async-start | bytes 3932160 | tf_op jit(solution)/shard_map/reduce_scatter | solution.py:386
  986.0 67.1 %copy-start.6 = (f32[4096,64]{0,1:T(8,128)S(1)}, f32[4096,64]{0,1:T(8,128)}, u32[]{:S(2)}) copy-start(f32[4096,64]{0,1:T(8,128)} %custom-call.1) | copy-start | bytes 3145732
  986.0 67.1 %copy-start.9 = (f32[4096,64]{0,1:T(8,128)S(1)}, f32[4096,64]{0,1:T(8,128)}, u32[]{:S(2)}) copy-start(f32[4096,64]{0,1:T(8,128)} %custom-call) | copy-start | bytes 3145732
  1119.8 78.0 %reduce-scatter.18.cloned.1.call-start = ((), (), s32[]{:S(2)}) async-start(), calls=%async_computation.22 | async-start | bytes 3932160 | tf_op jit(solution)/shard_map/reduce_scatter | solution.py:387
  1122.9 143.5 %reduce-scatter.30.cloned.1.call-start = ((), (), s32[]{:S(2)}) async-start(), calls=%async_computation.29 | async-start | bytes 442368
  1125.7 152.9 %reduce-scatter.28.cloned.1.call-start = ((), (), s32[]{:S(2)}) async-start(), calls=%async_computation.28 | async-start | bytes 2211840
  1206.6 195.9 %all-reduce.21.cloned.1.call-start = ((), (), s32[]{:S(2)}) async-start(), calls=%async_computation.23 | async-start | bytes 6291456 | tf_op jit(solution)/shard_map/psum | solution.py:415
  1211.6 368.4 %reduce-scatter.24.cloned.1.call-start = ((), (), s32[]{:S(2)}) async-start(), calls=%async_computation.26 | async-start | bytes 31457280 | tf_op jit(solution)/shard_map/reduce_scatter | solution.py:388
  1236.4 385.6 %reduce-scatter.32.cloned.1.call-start = ((), (), s32[]{:S(2)}) async-start(), calls=%async_computation.30 | async-start | bytes 1769472
  1243.0 428.9 %reduce-scatter.22.cloned.1.call-start = ((), (), s32[]{:S(2)}) async-start(), calls=%async_computation.25 | async-start | bytes 3538944 | tf_op jit(solution)/shard_map/reduce_scatter | solution.py:422
  1248.6 461.8 %reduce-scatter.20.cloned.1.call-start = ((), (), s32[]{:S(2)}) async-start(), calls=%async_computation.24 | async-start | bytes 884736 | tf_op jit(solution)/shard_map/reduce_scatter | solution.py:421
  1252.2 558.6 %reduce-scatter.26.cloned.1.call-start = ((), (), s32[]{:S(2)}) async-start(), calls=%async_computation.27 | async-start | bytes 15728640 | tf_op jit(solution)/shard_map/reduce_scatter | solution.py:389
  1265.7 140.3 %copy-start.104 = (f32[768]{0:T(1024)S(1)}, f32[768]{0:T(1024)}, u32[]{:S(2)}) copy-start(f32[768]{0:T(1024)} %get-tuple-element.853) | copy-start | bytes 9220
  1265.8 155.1 %copy-start.103 = (f32[1024]{0:T(1024)S(1)}, f32[1024]{0:T(1024)}, u32[]{:S(2)}) copy-start(f32[1024]{0:T(1024)} %copy-done.102) | copy-start | bytes 12292
  (128 other events, 1081.2 us)
Sparse Core Ops, SparseCore 0:
  44.1 20.4 all-gather.6
  66.7 19.6 all-gather.8
  147.5 121.0 all-reduce.14
  270.6 81.1 all-gather.10
  353.2 46.3 all-gather.12
  720.8 120.0 all-reduce.18
  843.8 67.8 all-reduce.16
  1119.9 36.8 reduce-scatter.15
  1159.9 37.7 reduce-scatter.17
  1200.6 33.8 reduce-scatter.29
  1238.5 40.1 reduce-scatter.27
  1281.5 121.0 all-reduce.20
  1405.2 174.7 reduce-scatter.23
  1583.7 38.3 reduce-scatter.31
  1625.8 46.0 reduce-scatter.21
  1675.5 34.9 reduce-scatter.19
  1713.4 97.2 reduce-scatter.25
Sparse Core Ops, SparseCore 1:
  471.3 32.2 all-gather.14
where the time goes:
time: 1830 us; the launch traced here: 1820 us
  waiting for transfers between devices  898 us (49%)
  matrix products  282 us (15%)
  local copies, waits for them, and re-layouts  247 us (13%)
  blocking collectives  193 us (11%)
  other arithmetic  150 us (8%)
  starting transfers between devices  27.3 us (1%)
  between operations  18.4 us (1%)
    reduce_scatter x1, waiting for transfers between devices, shards(): lax.psum_scatter(grad_ein, 'ctx', scatter_dimension=2, tiled=True)  152 us
    psum x1, waiting for transfers between devices, shards(): dnormed = lax.psum(dnormed, 'tensor')  122 us
    reduce_scatter x1, waiting for transfers between devices, shards(): lax.psum_scatter(grad_eout, 'ctx', scatter_dimension=1, tiled=True)  100 us
    all_gather x1, blocking collectives, shards(): lax.all_gather(shared_out, ('dp', 'ctx'), axis=0, tiled=True)  92.8 us
    psum x1, waiting for transfers between devices, shards(): branch = lax.psum(branch_part, 'tensor')  82.1 us
    psum x1, waiting for transfers between devices, shards(): lax.psum((combined + shared_part).astype(jnp.bfloat16), 'tensor')  64.7 us
    convert_element_type x6, other arithmetic, one_block(): dscores = (probs_full * (dprobs - delta_rows)).astype(jnp.bfloat16)  59.8 us
    all_to_all x1, waiting for transfers between devices, shards(): lax.all_to_all(row_grads, 'dp', split_axis=1, concat_axis=0, tiled=True)  58.2 us
  transfers between devices with their start and end apart: 22, of which 16 were waited for; matrix products, arithmetic and copies ran while one was open for 20% of the time, Pallas kernels for 0%

commit v1 on v0

v1 whole, which is shorter than its diff:
```python
import functools
import math

import jax
import jax.numpy as jnp
from jax import lax
from jax.experimental import pallas as pl
from jax.experimental.pallas import tpu as pltpu
from jax.sharding import PartitionSpec as P

HD = 64
HALF = HD // 2
EPSILON = 1e-06
LONGEST = 2000
DOCS = 5
BQ = 256
BK = 256
BF = jnp.bfloat16
F32 = jnp.float32
NEG = -1e30
DC = ("dp", "ctx")


def mm(a, b, ca, cb):
    return lax.dot_general(a, b, (((ca,), (cb,)), ((), ())), preferred_element_type=F32)


def attn_mask(scores_t, key_start, query_start, doc_row):
    rows, cols = scores_t.shape
    kpos = key_start + lax.broadcasted_iota(jnp.int32, (rows, cols), 0)
    qpos = query_start + lax.broadcasted_iota(jnp.int32, (rows, cols), 1)
    return (kpos <= qpos) & (kpos >= doc_row)


def attn_fwd_kernel(lo_ref, q_ref, k_ref, v_ref, doc_ref, o_ref, lse_ref, *, shift):
    rows = q_ref.shape[1]
    for qb in range(rows // BQ):
        qt = q_ref[:, qb * BQ : (qb + 1) * BQ]
        doc = doc_ref[:, qb * BQ : (qb + 1) * BQ]
        q0 = shift + qb * BQ

        def step(b, carry, qt=qt, doc=doc, q0=q0):
            peak, total, acc = carry
            off = pl.multiple_of(b * BK, BK)
            kt = k_ref[:, pl.ds(off, BK)]
            vt = v_ref[:, pl.ds(off, BK)]
            s = mm(kt, qt, 0, 0) * 0.125
            s = jnp.where(attn_mask(s, off, q0, doc), s, NEG)
            new = jnp.maximum(peak, jnp.max(s, axis=0, keepdims=True))
            p = jnp.exp(s - new)
            fix = jnp.exp(peak - new)
            total = total * fix + jnp.sum(p, axis=0, keepdims=True)
            acc = acc * fix + mm(vt, p.astype(BF), 1, 0)
            return new, total, acc

        init = (
            jnp.full((1, BQ), NEG, F32),
            jnp.zeros((1, BQ), F32),
            jnp.zeros((HD, BQ), F32),
        )
        last = (q0 + BQ - 1) // BK
        carry = step(last, init)
        peak, total, acc = lax.fori_loop(lo_ref[qb], last, step, carry)
        o_ref[:, qb * BQ : (qb + 1) * BQ] = (acc / total).astype(BF)
        lse_ref[0, :, qb * BQ : (qb + 1) * BQ] = peak + jnp.log(total)


def attn_bwd_kernel(
    lo_ref, q_ref, k_ref, v_ref, o_ref, do_ref, lse_ref, doc_ref, dq_ref, dk_ref, dv_ref, *, shift
):
    rows = q_ref.shape[1]
    dk_ref[...] = jnp.zeros_like(dk_ref)
    dv_ref[...] = jnp.zeros_like(dv_ref)
    for qb in range(rows // BQ):
        cols = slice(qb * BQ, (qb + 1) * BQ)
        qt = q_ref[:, cols]
        dot = do_ref[:, cols]
        doc = doc_ref[:, cols]
        lse = lse_ref[0, :, cols]
        delta = jnp.sum(dot.astype(F32) * o_ref[:, cols].astype(F32), axis=0, keepdims=True)
        q0 = shift + qb * BQ

        def step(b, dq, qt=qt, dot=dot, doc=doc, lse=lse, delta=delta, q0=q0):
            off = pl.multiple_of(b * BK, BK)
            kt = k_ref[:, pl.ds(off, BK)]
            vt = v_ref[:, pl.ds(off, BK)]
            s = mm(kt, qt, 0, 0) * 0.125
            s = jnp.where(attn_mask(s, off, q0, doc), s, NEG)
            p = jnp.exp(s - lse)
            dp = mm(vt, dot, 0, 0)
            ds = (p * (dp - delta)).astype(BF)
            dk_ref[:, pl.ds(off, BK)] += mm(qt, ds, 1, 1)
            dv_ref[:, pl.ds(off, BK)] += mm(dot, p.astype(BF), 1, 1)
            return dq + mm(kt, ds, 1, 0)

        last = (q0 + BQ - 1) // BK
        dq = lax.fori_loop(lo_ref[qb], last + 1, step, jnp.zeros((HD, BQ), F32))
        dq_ref[:, cols] = dq * 0.125
    dk_ref[...] = dk_ref[...] * 0.125


def head_spec(width):
    return pl.BlockSpec((HD, width), lambda h, lo: (h, 0))


def attn_forward(lo, q_t, k_t, v_t, doc, shift):
    cols, rows = q_t.shape
    window = k_t.shape[1]
    heads = cols // HD
    return pl.pallas_call(
        functools.partial(attn_fwd_kernel, shift=shift),
        out_shape=(
            jax.ShapeDtypeStruct((cols, rows), BF),
            jax.ShapeDtypeStruct((heads, 1, rows), F32),
        ),
        grid_spec=pltpu.PrefetchScalarGridSpec(
            num_scalar_prefetch=1,
            grid=(heads,),
            in_specs=[
                head_spec(rows),
                head_spec(window),
                head_spec(window),
                pl.BlockSpec((1, rows), lambda h, lo: (0, 0)),
            ],
            out_specs=[
                head_spec(rows),
                pl.BlockSpec((1, 1, rows), lambda h, lo: (h, 0, 0)),
            ],
        ),
        name="attn_fwd",
    )(lo, q_t, k_t, v_t, doc)


def attn_backward(lo, q_t, k_t, v_t, o_t, do_t, lse, doc, shift):
    cols, rows = q_t.shape
    window = k_t.shape[1]
    heads = cols // HD
    return pl.pallas_call(
        functools.partial(attn_bwd_kernel, shift=shift),
        out_shape=(
            jax.ShapeDtypeStruct((cols, rows), F32),
            jax.ShapeDtypeStruct((cols, window), F32),
            jax.ShapeDtypeStruct((cols, window), F32),
        ),
        grid_spec=pltpu.PrefetchScalarGridSpec(
            num_scalar_prefetch=1,
            grid=(heads,),
            in_specs=[
                head_spec(rows),
                head_spec(window),
                head_spec(window),
                head_spec(rows),
                head_spec(rows),
                pl.BlockSpec((1, 1, rows), lambda h, lo: (h, 0, 0)),
                pl.BlockSpec((1, rows), lambda h, lo: (0, 0)),
            ],
            out_specs=[head_spec(rows), head_spec(window), head_spec(window)],
        ),
        name="attn_bwd",
    )(lo, q_t, k_t, v_t, o_t, do_t, lse, doc)


def ffn_kernel(*refs, gated):
    if gated:
        x_ref, g_ref, gate_ref, win_ref, wout_ref = refs[:5]
        y_ref, dx_ref, dgate_ref, gin_ref, gout_ref, acc_in, acc_out = refs[5:]
    else:
        x_ref, g_ref, win_ref, wout_ref = refs[:4]
        y_ref, dx_ref, gin_ref, gout_ref, acc_in, acc_out = refs[4:]
    src, _, rows, width = x_ref.shape
    step = pl.program_id(1)

    @pl.when(step == 0)
    def _():
        acc_in[...] = jnp.zeros_like(acc_in)
        acc_out[...] = jnp.zeros_like(acc_out)

    x = x_ref[...].reshape(src * rows, width)
    g = g_ref[...].reshape(src * rows, width)
    w_gate = win_ref[0, 0]
    w_up = win_ref[0, 1]
    w_out = wout_ref[0]
    gate_pre = mm(x, w_gate, 1, 0)
    up_pre = mm(x, w_up, 1, 0)
    sig = 1.0 / (1.0 + jnp.exp(-gate_pre))
    silu = gate_pre * sig
    hidden = (silu * up_pre).astype(BF)
    y = mm(hidden, w_out, 1, 1)
    if gated:
        gf = g.astype(F32)
        gate = gate_ref[...].reshape(src * rows, 1)
        dgate_ref[...] = jnp.sum(gf * y, axis=1, keepdims=True).reshape(src, 1, rows, 1)
        dy = (gate * gf).astype(BF)
    else:
        dy = g
    y_ref[...] = y.astype(BF).reshape(src, 1, rows, width)
    dh = mm(dy, w_out, 1, 0)
    dgp = (dh * up_pre * (sig * (1.0 + gate_pre * (1.0 - sig)))).astype(BF)
    dup = (dh * silu).astype(BF)
    dx = mm(dgp, w_gate, 1, 1) + mm(dup, w_up, 1, 1)
    dx_ref[...] = dx.astype(BF).reshape(src, 1, rows, width)
    acc_in[0] += mm(x, dgp, 0, 0)
    acc_in[1] += mm(x, dup, 0, 0)
    acc_out[...] += mm(dy, hidden, 0, 0)

    @pl.when(step == pl.num_programs(1) - 1)
    def _():
        gin_ref[0] = acc_in[...].astype(BF)
        gout_ref[0] = acc_out[...].astype(BF)


def ffn(x, g, gate, w_in, w_out, block):
    sources, experts, rows, width = x.shape
    units = w_out.shape[2]
    gated = gate is not None
    block = math.gcd(sources, block)
    big = pl.BlockSpec((block, 1, rows, width), lambda e, s: (s, e, 0, 0))
    thin = pl.BlockSpec((block, 1, rows, 1), lambda e, s: (s, e, 0, 0))
    w_in_spec = pl.BlockSpec((1, 2, width, units), lambda e, s: (e, 0, 0, 0))
    w_out_spec = pl.BlockSpec((1, width, units), lambda e, s: (e, 0, 0))
    wide = jax.ShapeDtypeStruct(x.shape, BF)
    outs = [wide, wide]
    out_specs = [big, big]
    if gated:
        outs.append(jax.ShapeDtypeStruct(gate.shape, F32))
        out_specs.append(thin)
    outs += [
        jax.ShapeDtypeStruct((experts, 2, width, units), BF),
        jax.ShapeDtypeStruct((experts, width, units), BF),
    ]
    out_specs += [w_in_spec, w_out_spec]
    return pl.pallas_call(
        functools.partial(ffn_kernel, gated=gated),
        out_shape=outs,
        grid=(experts, sources // block),
        in_specs=[big, big] + ([thin] if gated else []) + [w_in_spec, w_out_spec],
        out_specs=out_specs,
        scratch_shapes=[
            pltpu.VMEM((2, width, units), F32),
            pltpu.VMEM((width, units), F32),
        ],
        compiler_params=pltpu.CompilerParams(
            dimension_semantics=("arbitrary", "arbitrary"), vmem_limit_bytes=56 * 1024 * 1024
        ),
        name="ffn_experts" if gated else "ffn_shared",
    )(*([x, g] + ([gate] if gated else []) + [w_in, w_out]))


def pair_slots(pair_route, order, experts, capacity):
    count = order.shape[0]
    flat = pair_route.reshape(count)
    number = jnp.arange(count, dtype=jnp.int32)
    ids = jnp.arange(experts, dtype=jnp.int32)
    owner = (flat[:, None] == ids[None, :]).astype(BF)
    ranked = jnp.dot(
        (order[:, None] == number[None, :]).astype(BF), owner, preferred_element_type=F32
    ).astype(BF)
    earlier = jnp.dot(
        (number[None, :] < number[:, None]).astype(BF), ranked, preferred_element_type=F32
    )
    ranked_slot = (jnp.minimum(earlier, float(capacity)) * ranked).astype(BF)
    slot = jnp.sum(
        jnp.dot(
            (order[None, :] == number[:, None]).astype(BF),
            ranked_slot,
            preferred_element_type=F32,
        ),
        axis=1,
    ).astype(jnp.int32)
    place = jnp.where(slot < capacity, flat * capacity + slot, experts * capacity)
    return place.reshape(pair_route.shape)


def own_sum(parts, axis):
    devices = lax.axis_size(DC)
    shape = parts.shape
    cut = shape[:axis] + (devices, shape[axis] // devices) + shape[axis + 1 :]
    swapped = lax.all_to_all(
        parts.astype(BF).reshape(cut), DC, split_axis=axis, concat_axis=axis, tiled=True
    )
    return jnp.sum(swapped.astype(F32), axis=axis)


def half_turn(values_t, cos_t, sin_t):
    cols, rows = values_t.shape
    split = values_t.reshape(cols // HD, 2, HALF, rows)
    a, b = split[:, 0], split[:, 1]
    return jnp.stack([a * cos_t - b * sin_t, b * cos_t + a * sin_t], axis=1).reshape(cols, rows)


def shards(
    tokens,
    segment_ids,
    routes,
    pair_order,
    gain_attn,
    qkv_weight,
    out_weight,
    gain_ffn,
    router_weight,
    shared_in,
    shared_out,
    expert_in,
    expert_out,
    out_grad,
):
    rows, width = tokens.shape[1], tokens.shape[2]
    ctx_count = lax.axis_size("ctx")
    ctx_at = lax.axis_index("ctx")
    inputs = tokens[0].astype(F32)
    grad_low = out_grad[0]
    grad_layer = grad_low.astype(F32)
    seg_all = segment_ids[0]
    my_routes = routes[0]

    gains = jnp.stack([gain_attn, gain_ffn], axis=1)
    heads_cols = qkv_weight.shape[2]
    experts = router_weight.shape[1]
    qkv_full = lax.all_gather(qkv_weight, DC, axis=1, tiled=True)
    rest = jnp.concatenate([out_weight, router_weight, gains], axis=1)
    gains_full = lax.all_gather(gains, DC, axis=0, tiled=True).astype(F32)
    rest_full = lax.all_gather(rest, DC, axis=0, tiled=True)
    out_full = rest_full[:, :heads_cols]
    router_full = rest_full[:, heads_cols : heads_cols + experts]
    attn_gain = gains_full[:, 0]
    ffn_gain = gains_full[:, 1]
    shin_full = lax.all_gather(shared_in, DC, axis=1, tiled=True)
    shout_full = lax.all_gather(shared_out, DC, axis=0, tiled=True)

    local_experts = expert_in.shape[0]
    spread = local_experts % ctx_count == 0
    if spread:
        expert_axes = DC
        ein = lax.all_to_all(expert_in, "ctx", split_axis=0, concat_axis=2, tiled=True)
        eout = lax.all_to_all(expert_out, "ctx", split_axis=0, concat_axis=1, tiled=True)
    else:
        expert_axes = ("dp",)
        ein = lax.all_gather(expert_in, "ctx", axis=2, tiled=True)
        eout = lax.all_gather(expert_out, "ctx", axis=1, tiled=True)
    owners = lax.axis_size(expert_axes)
    own = experts // owners
    capacity = 10 * rows // (4 * experts)
    slots = experts * capacity

    def swap(values):
        return lax.all_to_all(values, expert_axes, split_axis=0, concat_axis=0, tiled=True)

    place = pair_slots(my_routes, pair_order[0, 0], experts, capacity)
    slot_ids = jnp.arange(slots, dtype=jnp.int32)
    hit0 = place[None, :, 0] == slot_ids[:, None]
    hit1 = place[None, :, 1] == slot_ids[:, None]
    to_slot = (hit0 | hit1).astype(BF)
    slot_g = jnp.dot(to_slot, grad_low, preferred_element_type=F32).astype(BF)
    got_g = swap(slot_g.reshape(owners, own, capacity, width))

    inv1 = lax.rsqrt(jnp.mean(inputs * inputs, axis=-1, keepdims=True) + EPSILON)
    n1 = inputs * inv1
    normed = (n1 * attn_gain).astype(BF)
    row_start = ctx_at * rows
    query_pos = row_start + jnp.arange(rows, dtype=jnp.int32)
    inverse = 1.0 / 10000.0 ** (jnp.arange(HALF, dtype=F32) * (2.0 / HD))
    angles = inverse[:, None] * query_pos.astype(F32)[None, :]
    cos_t, sin_t = jnp.cos(angles), jnp.sin(angles)
    raw_t = jnp.einsum("pdc,ld->pcl", qkv_full, normed, preferred_element_type=F32)
    q_t = half_turn(raw_t[0], cos_t, sin_t).astype(BF)
    k_t = half_turn(raw_t[1], cos_t, sin_t).astype(BF)
    v_t = raw_t[2].astype(BF)
    kv_t = jnp.concatenate([k_t, v_t], axis=0)
    before = min(ctx_count - 1, -(-(LONGEST - 1) // rows))
    shift = before * rows
    pieces = [kv_t]
    for hop in range(1, before + 1):
        links = [(i, i + hop) for i in range(ctx_count - hop)]
        pieces.insert(0, lax.ppermute(kv_t, "ctx", links))
    kv_win = jnp.concatenate(pieces, axis=1)
    k_win, v_win = kv_win[:heads_cols], kv_win[heads_cols:]
    starts = jnp.sum(
        seg_all[:, None] < jnp.arange(DOCS, dtype=jnp.int32)[None, :], axis=0, dtype=jnp.int32
    )
    query_seg = lax.dynamic_slice_in_dim(seg_all, row_start, rows)
    doc = jnp.sum(
        jnp.where(
            query_seg[:, None] == jnp.arange(DOCS, dtype=jnp.int32)[None, :], starts[None, :], 0
        ),
        axis=1,
    ) - (row_start - shift)
    lo = jnp.maximum(doc[::BQ], 0) // BK
    doc = doc[None, :]
    att_t, lse = attn_forward(lo, q_t, k_win, v_win, doc, shift)
    branch_part = jnp.einsum("cl,dc->ld", att_t, out_full, preferred_element_type=F32)
    branch = lax.psum(branch_part.astype(BF), "tensor").astype(F32)
    resid = inputs + branch

    inv2 = lax.rsqrt(jnp.mean(resid * resid, axis=-1, keepdims=True) + EPSILON)
    n2 = resid * inv2
    normed2 = (n2 * ffn_gain).astype(BF)
    slot_x = jnp.dot(to_slot, normed2, preferred_element_type=F32).astype(BF)
    got_x = swap(slot_x.reshape(owners, own, capacity, width))
    logits = jnp.dot(normed2, router_full, preferred_element_type=F32)
    picked = my_routes[:, :, None] == jnp.arange(experts, dtype=jnp.int32)[None, None, :]
    chosen = jnp.sum(jnp.where(picked, logits[:, None, :], 0.0), axis=2)
    chosen_exp = jnp.exp(chosen - jnp.max(chosen, axis=1, keepdims=True))
    gates = chosen_exp / jnp.sum(chosen_exp, axis=1, keepdims=True)
    slot_gate = jnp.sum(
        jnp.where(hit0, gates[None, :, 0], 0.0) + jnp.where(hit1, gates[None, :, 1], 0.0), axis=1
    )
    got_gate = swap(slot_gate.reshape(owners, own * capacity))

    parts = 4
    shared_shape = (parts, 1, rows // parts, width)
    sh_y, sh_dx, sh_gin, sh_gout = ffn(
        normed2.reshape(shared_shape),
        grad_low.reshape(shared_shape),
        None,
        shin_full[None],
        shout_full[None],
        2,
    )
    total_shin = own_sum(sh_gin[0], 1)
    total_shout = own_sum(sh_gout[0], 0)

    y, dx, dgate, g_ein, g_eout = ffn(
        got_x, got_g, got_gate.reshape(owners, own, capacity, 1), ein, eout, 4
    )
    back_dx = swap(dx).reshape(slots, width)
    back_dgate = swap(dgate.reshape(owners, own * capacity)).reshape(slots)
    back_y = swap(y).reshape(slots, width)
    if spread:
        grad_ein = lax.all_to_all(g_ein, "ctx", split_axis=2, concat_axis=0, tiled=True)
        grad_eout = lax.all_to_all(g_eout, "ctx", split_axis=1, concat_axis=0, tiled=True)
    else:
        grad_ein = lax.psum_scatter(g_ein, "ctx", scatter_dimension=2, tiled=True)
        grad_eout = lax.psum_scatter(g_eout, "ctx", scatter_dimension=1, tiled=True)

    at0 = place[:, 0, None] == slot_ids[None, :]
    at1 = place[:, 1, None] == slot_ids[None, :]
    dn2_part = jnp.dot((at0 | at1).astype(BF), back_dx, preferred_element_type=F32)
    dgates = jnp.stack(
        [
            jnp.sum(jnp.where(at0, back_dgate[None, :], 0.0), axis=1),
            jnp.sum(jnp.where(at1, back_dgate[None, :], 0.0), axis=1),
        ],
        axis=1,
    )
    dchosen = gates * (dgates - jnp.sum(gates * dgates, axis=1, keepdims=True))
    dlogits = jnp.sum(jnp.where(picked, dchosen[:, :, None], 0.0), axis=1).astype(BF)
    dn2_part = (
        dn2_part
        + sh_dx.reshape(rows, width).astype(F32)
        + jnp.einsum("le,de->ld", dlogits, router_full, preferred_element_type=F32)
    )
    dn2 = lax.psum(dn2_part.astype(BF), "tensor").astype(F32)
    router_part = jnp.einsum("ld,le->de", normed2, dlogits, preferred_element_type=F32)
    gain2_part = jnp.sum(dn2_part * n2, axis=0)

    scaled2 = ffn_gain * dn2
    dresid = grad_layer + inv2 * (scaled2 - n2 * jnp.mean(scaled2 * n2, axis=-1, keepdims=True))
    dbranch = dresid.astype(BF)
    datt_t = jnp.einsum("dc,ld->cl", out_full, dbranch, preferred_element_type=F32).astype(BF)

    weight0 = jnp.where(at0, gates[:, 0, None], 0.0)
    weight1 = jnp.where(at1, gates[:, 1, None], 0.0)
    ffn_part = jnp.dot(
        (weight0 + weight1).astype(BF), back_y, preferred_element_type=F32
    ) + sh_y.reshape(rows, width).astype(F32)
    ffn_total = lax.psum(ffn_part.astype(BF), "tensor").astype(F32)
    layer_out = (resid + ffn_total).astype(BF)

    dq_t, dk_win, dv_win = attn_backward(
        lo, q_t, k_win, v_win, att_t, datt_t, lse, doc, shift
    )
    dkv_win = jnp.concatenate([dk_win, dv_win], axis=0)
    dkv = dkv_win[:, shift:]
    for hop in range(1, before + 1):
        links = [(i + hop, i) for i in range(ctx_count - hop)]
        piece = dkv_win[:, shift - hop * rows : shift - (hop - 1) * rows]
        dkv = dkv + lax.ppermute(piece.astype(BF), "ctx", links).astype(F32)
    dq_raw = half_turn(dq_t, cos_t, -sin_t)
    dk_raw = half_turn(dkv[:heads_cols], cos_t, -sin_t)
    draw_t = jnp.stack([dq_raw, dk_raw, dkv[heads_cols:]], axis=0).astype(BF)
    dn1_part = jnp.einsum("pcl,pdc->ld", draw_t, qkv_full, preferred_element_type=F32)
    dn1 = lax.psum(dn1_part.astype(BF), "tensor").astype(F32)
    gain1_part = jnp.sum(dn1_part * n1, axis=0)
    scaled1 = attn_gain * dn1
    grad_tokens = dresid + inv1 * (
        scaled1 - n1 * jnp.mean(scaled1 * n1, axis=-1, keepdims=True)
    )

    grad_qkv = jnp.einsum("ld,pcl->dpc", normed, draw_t, preferred_element_type=F32)
    grad_outw = jnp.einsum("ld,cl->dc", dbranch, att_t, preferred_element_type=F32)
    small = jnp.concatenate([router_part, gain1_part[:, None], gain2_part[:, None]], axis=1)
    tail = own_sum(
        jnp.concatenate([grad_qkv.reshape(width, 3 * heads_cols), grad_outw, small], axis=1), 0
    )
    total_qkv = tail[:, : 3 * heads_cols].reshape(-1, 3, heads_cols).transpose(1, 0, 2)
    total_outw = tail[:, 3 * heads_cols : 4 * heads_cols]
    small = lax.psum(tail[:, 4 * heads_cols :], "tensor")
    return (
        layer_out[None],
        grad_tokens[None],
        small[:, experts],
        total_qkv,
        total_outw,
        small[:, experts + 1],
        small[:, :experts],
        total_shin,
        total_shout,
        grad_ein.astype(F32),
        grad_eout.astype(F32),
    )


def solution(mesh):
    return jax.shard_map(
        shards,
        mesh=mesh,
        in_specs=(
            P("dp", "ctx", None),
            P("dp", None),
            P("dp", "ctx", None),
            P("dp", "ctx", None),
            P(DC),
            P(None, DC, "tensor"),
            P(DC, "tensor"),
            P(DC),
            P(DC, None),
            P(None, DC, "tensor"),
            P(DC, "tensor"),
            P("dp", None, "ctx", "tensor"),
            P("dp", "ctx", "tensor"),
            P("dp", "ctx", None),
        ),
        out_specs=(
            P("dp", "ctx", None),
            P("dp", "ctx", None),
            P(DC),
            P(None, DC, "tensor"),
            P(DC, "tensor"),
            P(DC),
            P(DC, None),
            P(None, DC, "tensor"),
            P(DC, "tensor"),
            P("dp", None, "ctx", "tensor"),
            P("dp", "ctx", "tensor"),
        ),
        check_vma=False,
    )
```

time: 1830 us -> 814 us (0.44)
  waiting for transfers between devices: 898 us -> 284 us
  matrix products: 282 us -> 63 us
  local copies, waits for them, and re-layouts: 247 us -> 67.4 us
  other arithmetic: 150 us -> 57.3 us
  Pallas kernels: 0 us -> 74.8 us
  starting transfers between devices: 27.3 us -> 95.3 us
  blocking collectives: 193 us -> 144 us
    reduce_scatter x6 -> x0, waiting for transfers between devices: 408 us -> none  [the longest x1 152 us: shards(): lax.psum_scatter(grad_ein, 'ctx', scatter_dimension=2, tiled=True)]
    dot_general x76 -> x14, matrix products: 280 us -> 60.7 us  [the longest x1 9.1 us: shards(): jnp.dot((weight0 + weight1).astype(BF), back_y, preferred_element_type=F32)]
    psum x4 -> x3, waiting for transfers between devices: 318 us -> 160 us  [the longest x1 73.3 us: shards(): ffn_total = lax.psum(ffn_part.astype(BF), 'tensor').astype(F32)]
    pallas_call x0 -> x4, Pallas kernels: none -> 74.8 us  [the longest x2 41.5 us: ffn(): pl.pallas_call(functools.partial(ffn_kernel, gated=gated), out_shape=outs...]
    gather x6 -> x0, local copies, waits for them, and re-layouts: 70.3 us -> none  [the longest x1 13.9 us: shards(): back_flat[pair_place].reshape(row_count, 2, send_width)]
    all_to_all x4 -> x11, starting transfers between devices: 25.4 us -> 85.9 us  [the longest x2 30.6 us: own_sum(): lax.all_to_all(parts.astype(BF).reshape(cut), DC, split_axis=axis, concat...]
    convert_element_type x13 -> x6, other arithmetic: 66.1 us -> 7.16 us  [the longest x1 4.08 us: shards(): grad_ein.astype(F32)]
    all_gather x4, blocking collectives: 155 us -> 102 us  [the longest x1 52 us: shards(): shout_full = lax.all_gather(shared_out, DC, axis=0, tiled=True)]
  transfers between devices with their start and end apart: 22 -> 19, of which waited for: 16 -> 9; matrix products, arithmetic and copies ran while one was open for 20% -> 18% of each run, Pallas kernels for 0% -> 7%
where the time goes in v1:
time: 814 us; the launch traced here: 803 us
  waiting for transfers between devices  284 us (35%)
  blocking collectives  144 us (18%)
  starting transfers between devices  95.3 us (12%)
  Pallas kernels  74.8 us (9%)
  local copies, waits for them, and re-layouts  67.4 us (8%)
  matrix products  63 us (8%)
  other arithmetic  57.3 us (7%)
  between operations  16.5 us (2%)
    all_to_all x5, waiting for transfers between devices, swap(): lax.all_to_all(values, expert_axes, split_axis=0, concat_axis=0, tiled=True)  77.4 us
    psum x1, waiting for transfers between devices, shards(): ffn_total = lax.psum(ffn_part.astype(BF), 'tensor').astype(F32)  73.3 us
    all_gather x1, blocking collectives, shards(): shout_full = lax.all_gather(shared_out, DC, axis=0, tiled=True)  52 us
    psum x1, waiting for transfers between devices, shards(): branch = lax.psum(branch_part.astype(BF), 'tensor').astype(F32)  46.2 us
    pallas_call x2, Pallas kernels, ffn(): pl.pallas_call(functools.partial(ffn_kernel, gated=gated), out_shape=outs...  41.5 us
    psum x1, waiting for transfers between devices, shards(): dn2 = lax.psum(dn2_part.astype(BF), 'tensor').astype(F32)  40.9 us
    all_to_all x2, starting transfers between devices, own_sum(): lax.all_to_all(parts.astype(BF).reshape(cut), DC, split_axis=axis, concat...  30.6 us
    all_gather x1, blocking collectives, shards(): rest_full = lax.all_gather(rest, DC, axis=0, tiled=True)  26.7 us
  transfers between devices with their start and end apart: 19, of which 9 were waited for; matrix products, arithmetic and copies ran while one was open for 18% of the time, Pallas kernels for 7%

profile of v1, /device:TPU:0, one launch (start us, length us, event | category | flops | bytes accessed | tf_op | source)
XLA Modules:
  0.0 802.8 jit_solution(9719048190512222659)
XLA Ops:
  8.9 10.3 %all-gather = bf16[8,96,2]{1,2,0:T(2,128)(2,1)S(1)} all-gather(bf16[1,96,2]{1,2,0:T(2,128)(2,1)S(1)} %maximum_bitcast_fusion), channel_id=1, replica_groups=mesh['dp'=2,'ctx'=4,'tensor'=4] {'dp','ctx'}, dimensions={0}, use_global_device_ids=true | all-gather | bytes 3456 | tf_op jit(solution)/shard_map/all_gather | solution.py:321
  22.1 13.3 %all_gather.16 = bf16[3,768,192]{2,0,1:T(4,128)(2,1)S(1)} all-gather(bf16[3,96,192]{2,0,1:T(4,128)(2,1)S(1)} %copy.168), channel_id=1, replica_groups=mesh['dp'=2,'ctx'=4,'tensor'=4] {'dp','ctx'}, dimensions={1}, use_global_device_ids=true | all-gather | bytes 995328 | tf_op jit(solution)/shard_map/all_gather | solution.py:319
  52.3 26.7 %all_gather.17 = bf16[768,210]{1,0:T(8,128)(2,1)S(1)} all-gather(bf16[96,210]{1,0:T(8,128)(2,1)S(1)} %pad_maximum_fusion.6), channel_id=1, replica_groups=mesh['dp'=2,'ctx'=4,'tensor'=4] {'dp','ctx'}, dimensions={0}, use_global_device_ids=true | all-gather | bytes 362880 | tf_op jit(solution)/shard_map/all_gather | solution.py:322
  83.5 15.6 %attn_fwd.1 = (bf16[192,1024]{1,0:T(8,128)(2,1)}, f32[3,1,1024]{2,1,0:T(1,128)}) custom-call(s32[4]{0:T(128)} %and_select_fusion.lo_ref, bf16[192,1024]{1,0:T(8,128)(2,1)} %bitcast.164, bf16[192,3072]{1,0:T(8,128)(2,1)} %get-tuple-element.133.k_ref, bf16[192,3072]{1,0:T(8,128)(2,1)} %get-tuple-element.132.v_ref, s32[1,1024]{1,0:T(1,128)} %bitcast.189), custom_call_target="tpu_custom_call" | custom-call | tf_op jit(solution)/shard_map/attn_fwd/pallas_call | solution.py:110
  101.9 19.2 %all-to-all-start.4 = ((bf16[8,192,512]{2,1,0:T(8,128)(2,1)}), bf16[8,192,512]{2,1,0:T(8,128)(2,1)}, u32[]{:S(2)}, u32[]{:S(2)}) async-start(bf16[8,192,512]{2,1,0:T(8,128)(2,1)} %param.26), calls=%async_computation.4 | async-start | bytes 3145728 | tf_op jit(solution)/shard_map/all_to_all | solution.py:335
  131.1 10.2 %all-to-all-done.4 = bf16[8,192,512]{2,1,0:T(8,128)(2,1)} async-done(((bf16[8,192,512]{2,1,0:T(8,128)(2,1)}), bf16[8,192,512]{2,1,0:T(8,128)(2,1)}, u32[]{:S(2)}, u32[]{:S(2)}) %all-to-all-start.4) | async-done | bytes 1572896 | tf_op jit(solution)/shard_map/all_to_all | solution.py:335
  141.3 4.8 all-to-all-start.3
  146.1 46.2 %all-reduce.5.cloned.1.call-done = bf16[1024,768]{1,0:T(8,128)(2,1)} async-done(((bf16[1024,768]{1,0:T(8,128)(2,1)}), bf16[1024,768]{1,0:T(8,128)(2,1)}) %all-reduce.5.cloned.1.call-update) | async-done | bytes 1572880 | tf_op jit(solution)/shard_map/psum | solution.py:391
  206.4 8.2 %fusion.28 = bf16[2560,768]{1,0:T(8,128)(2,1)} fusion(s32[1024]{0:T(1024)} %get-tuple-element.121, s32[1024]{0:T(1024)} %get-tuple-element.120, bf16[1,1024,768]{2,1,0:T(8,128)(2,1)} %param.27), kind=kOutput, calls=%fused_computation.35 | convolution fusion | flops 4036362240 | bytes 5513216 | tf_op jit(solution)/shard_map/dot_general | solution.py:353
  219.1 8.2 %fusion.25 = bf16[2560,768]{1,0:T(8,128)(2,1)} fusion(bf16[1024,768]{1,0:T(8,128)(2,1)} %copy-done.5, s32[1024]{0:T(1024)} %get-tuple-element.121, s32[1024]{0:T(1024)} %get-tuple-element.120), kind=kOutput, calls=%fused_computation.34 | convolution fusion | flops 4036362240 | bytes 5513216 | tf_op jit(solution)/shard_map/dot_general | solution.py:397
  227.3 37.2 %all-to-all-done.1.refs_1_ = bf16[8,2,160,768]{3,2,1,0:T(8,128)(2,1)} async-done(((bf16[8,2,160,768]{3,2,1,0:T(8,128)(2,1)}), bf16[8,2,160,768]{3,2,1,0:T(8,128)(2,1)}, u32[]{:S(2)}, u32[]{:S(2)}) %all-to-all-start.1) | async-done | bytes 3932192 | tf_op jit(solution)/shard_map/all_to_all | solution.py:346
  280.4 40.2 %all-to-all-done.refs_0_ = bf16[8,2,160,768]{3,2,1,0:T(8,128)(2,1)} async-done(((bf16[8,2,160,768]{3,2,1,0:T(8,128)(2,1)}), bf16[8,2,160,768]{3,2,1,0:T(8,128)(2,1)}, u32[]{:S(2)}, u32[]{:S(2)}) %all-to-all-start) | async-done | bytes 3932192 | tf_op jit(solution)/shard_map/all_to_all | solution.py:346
  320.7 28.4 %ffn_experts.1 = (bf16[8,2,160,768]{3,2,1,0:T(8,128)(2,1)}, bf16[8,2,160,768]{3,2,1,0:T(8,128)(2,1)}, f32[8,2,160,1]{3,2,1,0:T(8,128)}, bf16[2,2,768,512]{3,2,1,0:T(8,128)(2,1)}, bf16[2,768,512]{2,1,0:T(8,128)(2,1)}) custom-call(bf16[8,2,160,768]{3,2,1,0:T(8,128)(2,1)} %all-to-all-done.refs_0_, bf16[8,2,160,768]{3,2,1,0:T(8,128)(2,1)} %all-to-all-done.1.refs_1_, ...), custom_call_target="tpu_custom_call" | custom-call | tf_op jit(solution)/shard_map/ffn_experts/pallas_call | solution.py:232
  353.0 8.6 %all_to_all.108 = f32[8,1,320]{2,1,0:T(1,128)} all-to-all(f32[8,1,320]{2,1,0:T(1,128)} %all_to_all.94), channel_id=1, replica_groups=mesh['dp'=2,'ctx'=4,'tensor'=4] {'dp','ctx'}, dimensions={0} | all-to-all | bytes 20480 | tf_op jit(solution)/shard_map/all_to_all | solution.py:346
  366.2 52.0 %all_gather.19 = bf16[768,512]{1,0:T(8,128)(2,1)} all-gather(bf16[96,512]{1,0:T(8,128)(2,1)} %param.24), channel_id=1, replica_groups=mesh['dp'=2,'ctx'=4,'tensor'=4] {'dp','ctx'}, dimensions={0}, use_global_device_ids=true | all-gather | bytes 884736 | tf_op jit(solution)/shard_map/all_gather | solution.py:328
  418.2 13.1 %ffn_shared.1 = (bf16[4,1,256,768]{3,2,1,0:T(8,128)(2,1)}, bf16[4,1,256,768]{3,2,1,0:T(8,128)(2,1)}, bf16[1,2,768,512]{3,2,1,0:T(8,128)(2,1)}, bf16[1,768,512]{2,1,0:T(8,128)(2,1)}) custom-call(bf16[4,1,256,768]{3,2,1,0:T(8,128)(2,1)} %bitcast.154, bf16[4,1,256,768]{3,2,1,0:T(8,128)(2,1)} %bitcast.158, bf16[1,2,768,512]{3,2,1,0:T(8,128)(2,1)} %bitcast.181, ...), custom_call_target="tpu_custom_call" | custom-call | tf_op jit(solution)/shard_map/ffn_shared/pallas_call | solution.py:232
  439.6 7.6 fusion.5
  450.1 16.0 %all_to_all.109 = bf16[8,96,512]{2,1,0:T(8,128)(2,1)} all-to-all(bf16[8,96,512]{2,1,0:T(8,128)(2,1)} %bitcast.186), channel_id=1, replica_groups=mesh['dp'=2,'ctx'=4,'tensor'=4] {'dp','ctx'}, dimensions={0} | all-to-all | bytes 1572864 | tf_op jit(solution)/shard_map/all_to_all | solution.py:278
  466.1 4.7 all-to-all-start.5
  476.5 40.9 %all-reduce.7.cloned.1.call-done = bf16[1024,768]{1,0:T(8,128)(2,1)} async-done(((bf16[1024,768]{1,0:T(8,128)(2,1)}), bf16[1024,768]{1,0:T(8,128)(2,1)}) %all-reduce.7.cloned.1.call-update) | async-done | bytes 1572880 | tf_op jit(solution)/shard_map/psum | solution.py:452
  525.5 17.7 %attn_bwd.1 = (f32[192,1024]{1,0:T(8,128)}, f32[192,3072]{1,0:T(8,128)}, f32[192,3072]{1,0:T(8,128)}) custom-call(s32[4]{0:T(128)} %and_select_fusion.lo_ref, bf16[192,1024]{1,0:T(8,128)(2,1)} %bitcast.165, bf16[192,3072]{1,0:T(8,128)(2,1)} %get-tuple-element.133.k_ref, bf16[192,3072]{1,0:T(8,128)(2,1)} %get-tuple-element.132.v_ref, ...), custom_call_target="tpu_custom_call" | custom-call | tf_op jit(solution)/shard_map/attn_bwd/pallas_call | solution.py:138
  551.7 26.0 %all-to-all-start.9 = ((bf16[2,8,96,512]{3,2,0,1:T(8,128)(2,1)}), bf16[2,8,96,512]{3,2,0,1:T(8,128)(2,1)}, u32[]{:S(2)}, u32[]{:S(2)}) async-start(bf16[2,8,96,512]{3,2,0,1:T(8,128)(2,1)} %copy.187), calls=%async_computation.9 | async-start | bytes 3145728 | tf_op jit(solution)/shard_map/all_to_all | solution.py:278
  577.8 9.1 %fusion.49 = bf16[1024,768]{1,0:T(8,128)(2,1)} fusion(bf16[1024,768]{1,0:T(8,128)(2,1)} %bitcast.205, bf16[2560,768]{1,0:T(8,128)(2,1)} %bitcast.30, f32[1024]{0:T(1024)S(1)} %bitcast.200, s32[1024]{0:T(1024)S(1)} %copy-done.36, f32[1024]{0:T(1024)S(1)} %bitcast.198, s32[1024]{0:T(1024)S(1)} %copy-done.35), kind=kOutput, calls=%fused_computation.59 | convolution fusion | flops 4044619776 | bytes 7094272 | tf_op jit(solution)/shard_map/dot_general | solution.py:463
  586.9 21.8 %collective-permute-done.3 = bf16[384,1024]{1,0:T(8,128)(2,1)} collective-permute-done((bf16[384,1024]{1,0:T(8,128)(2,1)}, bf16[384,1024]{1,0:T(8,128)(2,1)}, u32[]{:S(2)}, u32[]{:S(2)}) %collective-permute-start.3) | collective-permute-done | bytes 786464 | tf_op jit(solution)/shard_map/ppermute | solution.py:477
  617.6 5.1 bitcast_convert_fusion
  622.7 6.7 copy.188
  629.4 8.0 all-to-all-done.12
  637.4 4.7 all-to-all-start.11
  669.3 73.3 %all-reduce.9.cloned.1.call-done = (bf16[1024,768]{1,0:T(8,128)(2,1)}, bf16[1024,768]{1,0:T(8,128)(2,1)}) async-done(((bf16[1024,768]{1,0:T(8,128)(2,1)}, bf16[1024,768]{1,0:T(8,128)(2,1)}), (bf16[1024,768]{1,0:T(8,128)(2,1)}, bf16[1024,768]{1,0:T(8,128)(2,1)})) %all-reduce.9.cloned.1.call-update) | async-done | bytes 3145744 | tf_op jit(solution)/shard_map/psum | solution.py:466
  759.5 4.6 copy.189
  767.2 6.2 all-to-all-done.8
  776.8 17.1 %psum.39 = f32[96,18]{1,0:T(8,128)S(1)} all-reduce(f32[96,18]{1,0:T(8,128)S(1)} %slice.166), channel_id=1, replica_groups=mesh['dp'=2,'ctx'=4,'tensor'=4] {'tensor'}, use_global_device_ids=true, to_apply=%region_22.23 | all-reduce | flops 1728 | bytes 13824 | tf_op jit(solution)/shard_map/psum | solution.py:497
  (224 shorter events, 174.5 us)
Async XLA Ops:
  8.0 29.5 %copy-start = (bf16[1,1024,768]{2,1,0:T(8,128)(2,1)S(1)}, bf16[1,1024,768]{2,1,0:T(8,128)(2,1)}, u32[]{:S(2)}) copy-start(bf16[1,1024,768]{2,1,0:T(8,128)(2,1)} %param.14) | copy-start | bytes 4718596
  8.0 184.3 %all-reduce.5.cloned.1.call-start = ((), (), s32[]{:S(2)}) async-start(), calls=%async_computation.13 | async-start | bytes 3145728 | tf_op jit(solution)/shard_map/psum | solution.py:391
  19.3 175.2 %copy-start.23 = (f32[768]{0:T(1024)}, f32[768]{0:T(1024)S(1)}, u32[]{:S(2)}) copy-start(f32[768]{0:T(1024)S(1)} %get-tuple-element.126) | copy-start | bytes 9220
  42.2 37.6 %copy-start.16 = (f32[32,1024]{1,0:T(8,128)}, f32[32,1024]{1,0:T(8,128)S(1)}, u32[]{:S(2)}) copy-start(f32[32,1024]{1,0:T(8,128)S(1)} %get-tuple-element.154) | copy-start | bytes 393220
  44.3 34.8 %copy-start.18 = (bf16[3,1,32,1024]{3,2,1,0:T(8,128)(2,1)S(1)}, bf16[3,1,32,1024]{3,2,1,0:T(8,128)(2,1)}, u32[]{:S(2)}) copy-start(bf16[3,1,32,1024]{3,2,1,0:T(8,128)(2,1)} %get-tuple-element.149) | copy-start | bytes 589828
  45.3 35.1 %collective-permute-start = (bf16[384,1024]{1,0:T(8,128)(2,1)}, bf16[384,1024]{1,0:T(8,128)(2,1)}, u32[]{:S(2)}, u32[]{:S(2)}) collective-permute-start(bf16[384,1024]{1,0:T(8,128)(2,1)} %pad_maximum_fusion.1), channel_id=1, source_target_pairs={{0,8},{4,12},{1,9},{5,13},{2,10},{6,14},{3,11},{7,15},{16,24},{20,... | collective-permute-start | bytes 2359304 | tf_op jit(solution)/shard_map/ppermute | solution.py:374
  48.6 31.8 %collective-permute-start.1 = (bf16[384,1024]{1,0:T(8,128)(2,1)}, bf16[384,1024]{1,0:T(8,128)(2,1)}, u32[]{:S(2)}, u32[]{:S(2)}) collective-permute-start(bf16[384,1024]{1,0:T(8,128)(2,1)} %pad_maximum_fusion.1), channel_id=1, source_target_pairs={{0,4},{4,8},{8,12},{1,5},{5,9},{9,13},{2,6},{6,10},{10,14},{3,7},{... | collective-permute-start | bytes 2359304 | tf_op jit(solution)/shard_map/ppermute | solution.py:374
  52.0 31.5 %copy-start.32 = (s32[1024]{0:T(1024)}, s32[1024]{0:T(1024)S(1)}, u32[]{:S(2)}) copy-start(s32[1024]{0:T(1024)S(1)} %broadcast_subtract_fusion) | copy-start | bytes 12292
  101.9 39.4 %all-to-all-start.4 = ((bf16[8,192,512]{2,1,0:T(8,128)(2,1)}), bf16[8,192,512]{2,1,0:T(8,128)(2,1)}, u32[]{:S(2)}, u32[]{:S(2)}) async-start(bf16[8,192,512]{2,1,0:T(8,128)(2,1)} %param.26), calls=%async_computation.4 | async-start | bytes 3145728 | tf_op jit(solution)/shard_map/all_to_all | solution.py:335
  121.9 74.9 %copy-start.22 = (s32[1024,2]{0,1:T(2,128)}, s32[1024,2]{0,1:T(2,128)S(1)}, u32[]{:S(2)}) copy-start(s32[1024,2]{0,1:T(2,128)S(1)} %copy.175) | copy-start | bytes 24580
  141.3 61.1 %all-to-all-start.3 = ((bf16[8,2,192,512]{3,2,1,0:T(8,128)(2,1)}), bf16[8,2,192,512]{3,2,1,0:T(8,128)(2,1)}, u32[]{:S(2)}, u32[]{:S(2)}) async-start(bf16[8,2,192,512]{3,2,1,0:T(8,128)(2,1)} %param.25), calls=%async_computation.3 | async-start | bytes 6291456 | tf_op jit(solution)/shard_map/all_to_all | solution.py:334
  202.4 12.2 %all-to-all-start.2 = ((f32[8,1,320]{2,1,0:T(1,128)}), f32[8,1,320]{2,1,0:T(1,128)}, u32[]{:S(2)}, u32[]{:S(2)}) async-start(f32[8,1,320]{2,1,0:T(1,128)} %all_to_all.75), calls=%async_computation.2 | async-start | bytes 24576 | tf_op jit(solution)/shard_map/all_to_all | solution.py:346
  214.6 49.9 %all-to-all-start.1 = ((bf16[8,2,160,768]{3,2,1,0:T(8,128)(2,1)}), bf16[8,2,160,768]{3,2,1,0:T(8,128)(2,1)}, u32[]{:S(2)}, u32[]{:S(2)}) async-start(bf16[8,2,160,768]{3,2,1,0:T(8,128)(2,1)} %bitcast.161), calls=%async_computation.1 | async-start | bytes 7864320 | tf_op jit(solution)/shard_map/all_to_all | solution.py:346
  264.5 56.2 %all-to-all-start = ((bf16[8,2,160,768]{3,2,1,0:T(8,128)(2,1)}), bf16[8,2,160,768]{3,2,1,0:T(8,128)(2,1)}, u32[]{:S(2)}, u32[]{:S(2)}) async-start(bf16[8,2,160,768]{3,2,1,0:T(8,128)(2,1)} %bitcast.160), calls=%async_computation | async-start | bytes 7864320 | tf_op jit(solution)/shard_map/all_to_all | solution.py:346
  269.0 149.2 %all-gather.3.cloned.1.call-start = ((), (), s32[]{:S(2)}) async-start(), calls=%async_computation.14 | async-start | bytes 1769472 | tf_op jit(solution)/shard_map/all_gather | solution.py:327
  361.6 78.0 %all-to-all-start.6 = ((bf16[8,2,160,768]{3,2,1,0:T(8,128)(2,1)}), bf16[8,2,160,768]{3,2,1,0:T(8,128)(2,1)}, u32[]{:S(2)}, u32[]{:S(2)}) async-start(bf16[8,2,160,768]{3,2,1,0:T(8,128)(2,1)} %get-tuple-element.28), calls=%async_computation.6 | async-start | bytes 7864320 | tf_op jit(solution)/shard_map/all_to_all | solution.py:346
  366.1 151.3 %all-reduce.7.cloned.1.call-start = ((), (), s32[]{:S(2)}) async-start(), calls=%async_computation.15 | async-start | bytes 3145728 | tf_op jit(solution)/shard_map/psum | solution.py:452
  466.1 85.7 %all-to-all-start.5 = ((bf16[8,2,160,768]{3,2,1,0:T(8,128)(2,1)}), bf16[8,2,160,768]{3,2,1,0:T(8,128)(2,1)}, u32[]{:S(2)}, u32[]{:S(2)}) async-start(bf16[8,2,160,768]{3,2,1,0:T(8,128)(2,1)} %get-tuple-element.26), calls=%async_computation.5 | async-start | bytes 7864320 | tf_op jit(solution)/shard_map/all_to_all | solution.py:346
  470.8 46.6 %copy-start.24 = (f32[768]{0:T(1024)S(1)}, f32[768]{0:T(1024)}, u32[]{:S(2)}) copy-start(f32[768]{0:T(1024)} %copy-done.23) | copy-start | bytes 9220
  470.8 46.6 %copy-start.26 = (f32[1024]{0:T(1024)S(1)}, f32[1024]{0:T(1024)}, u32[]{:S(2)}) copy-start(f32[1024]{0:T(1024)} %copy-done.25) | copy-start | bytes 12292
  547.9 29.9 %copy-start.35 = (s32[1024]{0:T(1024)S(1)}, s32[1024]{0:T(1024)}, u32[]{:S(2)}) copy-start(s32[1024]{0:T(1024)} %get-tuple-element.120) | copy-start | bytes 12292
  547.9 29.9 %copy-start.36 = (s32[1024]{0:T(1024)S(1)}, s32[1024]{0:T(1024)}, u32[]{:S(2)}) copy-start(s32[1024]{0:T(1024)} %get-tuple-element.121) | copy-start | bytes 12292
  547.9 29.9 %copy-start.39 = (f32[1024,1]{0,1:T(1,128)S(1)}, f32[1024,1]{0,1:T(1,128)}, u32[]{:S(2)}) copy-start(f32[1024,1]{0,1:T(1,128)} %copy-done.38) | copy-start | bytes 12292
  547.9 29.9 %copy-start.41 = (f32[1024,1]{0,1:T(1,128)S(1)}, f32[1024,1]{0,1:T(1,128)}, u32[]{:S(2)}) copy-start(f32[1024,1]{0,1:T(1,128)} %copy-done.40) | copy-start | bytes 12292
  549.1 37.8 %collective-permute-start.2 = (bf16[384,1024]{1,0:T(8,128)(2,1)}, bf16[384,1024]{1,0:T(8,128)(2,1)}, u32[]{:S(2)}, u32[]{:S(2)}) collective-permute-start(bf16[384,1024]{1,0:T(8,128)(2,1)} %get-tuple-element.130), channel_id=1, source_target_pairs={{4,0},{8,4},{12,8},{5,1},{9,5},{13,9},{6,2},{10,6},{14,10},{7,3},{... | collective-permute-start | bytes 2359304 | tf_op jit(solution)/shard_map/ppermute | solution.py:477
  550.4 58.3 %collective-permute-start.3 = (bf16[384,1024]{1,0:T(8,128)(2,1)}, bf16[384,1024]{1,0:T(8,128)(2,1)}, u32[]{:S(2)}, u32[]{:S(2)}) collective-permute-start(bf16[384,1024]{1,0:T(8,128)(2,1)} %get-tuple-element.131), channel_id=1, source_target_pairs={{8,0},{12,4},{9,1},{13,5},{10,2},{14,6},{11,3},{15,7},{24,16},{28,... | collective-permute-start | bytes 2359304 | tf_op jit(solution)/shard_map/ppermute | solution.py:477
  551.7 61.2 %all-to-all-start.9 = ((bf16[2,8,96,512]{3,2,0,1:T(8,128)(2,1)}), bf16[2,8,96,512]{3,2,0,1:T(8,128)(2,1)}, u32[]{:S(2)}, u32[]{:S(2)}) async-start(bf16[2,8,96,512]{3,2,0,1:T(8,128)(2,1)} %copy.187), calls=%async_computation.9 | async-start | bytes 3145728 | tf_op jit(solution)/shard_map/all_to_all | solution.py:278
  586.9 24.1 %copy-start.20 = (f32[32,1024]{1,0:T(8,128)S(1)}, f32[32,1024]{1,0:T(8,128)}, u32[]{:S(2)}) copy-start(f32[32,1024]{1,0:T(8,128)} %get-tuple-element.152) | copy-start | bytes 393220
  612.9 24.5 %all-to-all-start.12 = ((bf16[2,768,512]{2,0,1:T(2,128)(2,1)}), bf16[2,768,512]{2,0,1:T(2,128)(2,1)}, u32[]{:S(2)}, u32[]{:S(2)}) async-start(bf16[2,768,512]{2,0,1:T(2,128)(2,1)} %copy.190), calls=%async_computation.12 | async-start | bytes 3145728 | tf_op jit(solution)/shard_map/all_to_all | solution.py:430
  617.3 125.3 %all-reduce.9.cloned.1.call-start = ((), (), s32[]{:S(2)}) async-start(), calls=%async_computation.16 | async-start | bytes 6291456 | tf_op jit(solution)/shard_map/psum | solution.py:466
  637.4 113.4 %all-to-all-start.11 = ((bf16[2,2,768,512]{3,1,0,2:T(2,128)(2,1)}), bf16[2,2,768,512]{3,1,0,2:T(2,128)(2,1)}, u32[]{:S(2)}, u32[]{:S(2)}) async-start(bf16[2,2,768,512]{3,1,0,2:T(2,128)(2,1)} %copy.188), calls=%async_computation.11 | async-start | bytes 6291456 | tf_op jit(solution)/shard_map/all_to_all | solution.py:429
  750.9 22.5 %all-to-all-start.8 = ((bf16[8,96,786]{2,1,0:T(8,128)(2,1)}), bf16[8,96,786]{2,1,0:T(8,128)(2,1)}, u32[]{:S(2)}, u32[]{:S(2)}) async-start(bf16[8,96,786]{2,1,0:T(8,128)(2,1)} %concatenate.38), calls=%async_computation.8 | async-start | bytes 2752512 | tf_op jit(solution)/shard_map/all_to_all | solution.py:278
  (32 other events, 270.9 us)
Sparse Core Ops, SparseCore 0:
  102.0 90.2 all-reduce.4
  450.2 67.1 all-reduce.6
  622.8 119.7 all-reduce.8
Sparse Core Ops, SparseCore 1:
  271.4 44.7 all-gather.2

commit v2 on v1

--- a/solution.py
+++ b/solution.py
@@ -246,6 +246,10 @@
     )(*([x, g] + ([gate] if gated else []) + [w_in, w_out]))
 
 
+def after(value, *first):
+    return lax.optimization_barrier((value,) + first)[0]
+
+
 def pair_slots(pair_route, order, experts, capacity):
     count = order.shape[0]
     flat = pair_route.reshape(count)
@@ -313,30 +317,29 @@
     seg_all = segment_ids[0]
     my_routes = routes[0]
 
-    gains = jnp.stack([gain_attn, gain_ffn], axis=1)
     heads_cols = qkv_weight.shape[2]
+    qkv_cols = 3 * heads_cols
     experts = router_weight.shape[1]
-    qkv_full = lax.all_gather(qkv_weight, DC, axis=1, tiled=True)
-    rest = jnp.concatenate([out_weight, router_weight, gains], axis=1)
-    gains_full = lax.all_gather(gains, DC, axis=0, tiled=True).astype(F32)
-    rest_full = lax.all_gather(rest, DC, axis=0, tiled=True)
-    out_full = rest_full[:, :heads_cols]
-    router_full = rest_full[:, heads_cols : heads_cols + experts]
-    attn_gain = gains_full[:, 0]
-    ffn_gain = gains_full[:, 1]
-    shin_full = lax.all_gather(shared_in, DC, axis=1, tiled=True)
-    shout_full = lax.all_gather(shared_out, DC, axis=0, tiled=True)
+    thin = jnp.concatenate(
+        [
+            qkv_weight.transpose(1, 0, 2).reshape(-1, qkv_cols),
+            out_weight,
+            router_weight,
+            gain_attn[:, None],
+            gain_ffn[:, None],
+        ],
+        axis=1,
+    )
+    thin_full = lax.all_gather(thin, DC, axis=0, tiled=True)
+    qkv_full = thin_full[:, :qkv_cols]
+    out_full = thin_full[:, qkv_cols : qkv_cols + heads_cols]
+    router_full = thin_full[:, qkv_cols + heads_cols : qkv_cols + heads_cols + experts]
+    attn_gain = thin_full[:, -2].astype(F32)
+    ffn_gain = thin_full[:, -1].astype(F32)
 
     local_experts = expert_in.shape[0]
     spread = local_experts % ctx_count == 0
-    if spread:
-        expert_axes = DC
-        ein = lax.all_to_all(expert_in, "ctx", split_axis=0, concat_axis=2, tiled=True)
-        eout = lax.all_to_all(expert_out, "ctx", split_axis=0, concat_axis=1, tiled=True)
-    else:
-        expert_axes = ("dp",)
-        ein = lax.all_gather(expert_in, "ctx", axis=2, tiled=True)
-        eout = lax.all_gather(expert_out, "ctx", axis=1, tiled=True)
+    expert_axes = DC if spread else ("dp",)
     owners = lax.axis_size(expert_axes)
     own = experts // owners
     capacity = 10 * rows // (4 * experts)
@@ -351,7 +354,6 @@
     hit1 = place[None, :, 1] == slot_ids[:, None]
     to_slot = (hit0 | hit1).astype(BF)
     slot_g = jnp.dot(to_slot, grad_low, preferred_element_type=F32).astype(BF)
-    got_g = swap(slot_g.reshape(owners, own, capacity, width))
 
     inv1 = lax.rsqrt(jnp.mean(inputs * inputs, axis=-1, keepdims=True) + EPSILON)
     n1 = inputs * inv1
@@ -361,10 +363,10 @@
     inverse = 1.0 / 10000.0 ** (jnp.arange(HALF, dtype=F32) * (2.0 / HD))
     angles = inverse[:, None] * query_pos.astype(F32)[None, :]
     cos_t, sin_t = jnp.cos(angles), jnp.sin(angles)
-    raw_t = jnp.einsum("pdc,ld->pcl", qkv_full, normed, preferred_element_type=F32)
-    q_t = half_turn(raw_t[0], cos_t, sin_t).astype(BF)
-    k_t = half_turn(raw_t[1], cos_t, sin_t).astype(BF)
-    v_t = raw_t[2].astype(BF)
+    raw_t = jnp.einsum("dc,ld->cl", qkv_full, normed, preferred_element_type=F32)
+    q_t = half_turn(raw_t[:heads_cols], cos_t, sin_t).astype(BF)
+    k_t = half_turn(raw_t[heads_cols : 2 * heads_cols], cos_t, sin_t).astype(BF)
+    v_t = raw_t[2 * heads_cols :].astype(BF)
     kv_t = jnp.concatenate([k_t, v_t], axis=0)
     before = min(ctx_count - 1, -(-(LONGEST - 1) // rows))
     shift = before * rows
@@ -374,6 +376,18 @@
         pieces.insert(0, lax.ppermute(kv_t, "ctx", links))
     kv_win = jnp.concatenate(pieces, axis=1)
     k_win, v_win = kv_win[:heads_cols], kv_win[heads_cols:]
+
+    expert_in, expert_out, slot_g, _ = lax.optimization_barrier(
+        (expert_in, expert_out, slot_g, kv_win)
+    )
+    if spread:
+        ein = lax.all_to_all(expert_in, "ctx", split_axis=0, concat_axis=2, tiled=True)
+        eout = lax.all_to_all(expert_out, "ctx", split_axis=0, concat_axis=1, tiled=True)
+    else:
+        ein = lax.all_gather(expert_in, "ctx", axis=2, tiled=True)
+        eout = lax.all_gather(expert_out, "ctx", axis=1, tiled=True)
+    got_g = swap(slot_g.reshape(owners, own, capacity, width))
+
     starts = jnp.sum(
         seg_all[:, None] < jnp.arange(DOCS, dtype=jnp.int32)[None, :], axis=0, dtype=jnp.int32
     )
@@ -388,7 +402,9 @@
     doc = doc[None, :]
     att_t, lse = attn_forward(lo, q_t, k_win, v_win, doc, shift)
     branch_part = jnp.einsum("cl,dc->ld", att_t, out_full, preferred_element_type=F32)
-    branch = lax.psum(branch_part.astype(BF), "tensor").astype(F32)
+    branch = lax.psum(branch_part.astype(BF), "tensor")
+    branch, ein, eout, got_g = lax.optimization_barrier((branch, ein, eout, got_g))
+    branch = branch.astype(F32)
     resid = inputs + branch
 
     inv2 = lax.rsqrt(jnp.mean(resid * resid, axis=-1, keepdims=True) + EPSILON)
@@ -406,31 +422,25 @@
     )
     got_gate = swap(slot_gate.reshape(owners, own * capacity))
 
+    shared_w = after(jnp.concatenate([shared_in, shared_out[None]], axis=0), got_x)
+    shared_full = lax.all_gather(shared_w, DC, axis=1, tiled=True)
+    y, dx, dgate, g_ein, g_eout = ffn(
+        got_x, got_g, got_gate.reshape(owners, own, capacity, 1), ein, eout, 4
+    )
+    back_dx = swap(dx).reshape(slots, width)
+    back_dgate = swap(dgate.reshape(owners, own * capacity)).reshape(slots)
+
     parts = 4
     shared_shape = (parts, 1, rows // parts, width)
     sh_y, sh_dx, sh_gin, sh_gout = ffn(
         normed2.reshape(shared_shape),
         grad_low.reshape(shared_shape),
         None,
-        shin_full[None],
-        shout_full[None],
+        shared_full[None, :2],
+        shared_full[None, 2],
         2,
     )
-    total_shin = own_sum(sh_gin[0], 1)
-    total_shout = own_sum(sh_gout[0], 0)
-
-    y, dx, dgate, g_ein, g_eout = ffn(
-        got_x, got_g, got_gate.reshape(owners, own, capacity, 1), ein, eout, 4
-    )
-    back_dx = swap(dx).reshape(slots, width)
-    back_dgate = swap(dgate.reshape(owners, own * capacity)).reshape(slots)
-    back_y = swap(y).reshape(slots, width)
-    if spread:
-        grad_ein = lax.all_to_all(g_ein, "ctx", split_axis=2, concat_axis=0, tiled=True)
-        grad_eout = lax.all_to_all(g_eout, "ctx", split_axis=1, concat_axis=0, tiled=True)
-    else:
-        grad_ein = lax.psum_scatter(g_ein, "ctx", scatter_dimension=2, tiled=True)
-        grad_eout = lax.psum_scatter(g_eout, "ctx", scatter_dimension=1, tiled=True)
+    back_dx, sh_dx = lax.optimization_barrier((back_dx, sh_dx))
 
     at0 = place[:, 0, None] == slot_ids[None, :]
     at1 = place[:, 1, None] == slot_ids[None, :]
@@ -449,7 +459,19 @@
         + sh_dx.reshape(rows, width).astype(F32)
         + jnp.einsum("le,de->ld", dlogits, router_full, preferred_element_type=F32)
     )
-    dn2 = lax.psum(dn2_part.astype(BF), "tensor").astype(F32)
+    dn2_low = dn2_part.astype(BF)
+    back_y = swap(after(y, dn2_low)).reshape(slots, width)
+    dn2 = lax.psum(dn2_low, "tensor")
+    dn2, back_y = lax.optimization_barrier((dn2, back_y))
+    g_eout, sh_grad, _ = lax.optimization_barrier(
+        (g_eout, jnp.concatenate([sh_gin[0], sh_gout], axis=0), dn2)
+    )
+    if spread:
+        grad_eout = lax.all_to_all(g_eout, "ctx", split_axis=1, concat_axis=0, tiled=True)
+    else:
+        grad_eout = lax.psum_scatter(g_eout, "ctx", scatter_dimension=1, tiled=True)
+    total_shared = own_sum(sh_grad, 1)
+    dn2 = dn2.astype(F32)
     router_part = jnp.einsum("ld,le->de", normed2, dlogits, preferred_element_type=F32)
     gain2_part = jnp.sum(dn2_part * n2, axis=0)
 
@@ -463,8 +485,8 @@
     ffn_part = jnp.dot(
         (weight0 + weight1).astype(BF), back_y, preferred_element_type=F32
     ) + sh_y.reshape(rows, width).astype(F32)
-    ffn_total = lax.psum(ffn_part.astype(BF), "tensor").astype(F32)
-    layer_out = (resid + ffn_total).astype(BF)
+    ffn_low, datt_t = lax.optimization_barrier((ffn_part.astype(BF), datt_t))
+    ffn_total = lax.psum(ffn_low, "tensor")
 
     dq_t, dk_win, dv_win = attn_backward(
         lo, q_t, k_win, v_win, att_t, datt_t, lse, doc, shift
@@ -477,24 +499,33 @@
         dkv = dkv + lax.ppermute(piece.astype(BF), "ctx", links).astype(F32)
     dq_raw = half_turn(dq_t, cos_t, -sin_t)
     dk_raw = half_turn(dkv[:heads_cols], cos_t, -sin_t)
-    draw_t = jnp.stack([dq_raw, dk_raw, dkv[heads_cols:]], axis=0).astype(BF)
-    dn1_part = jnp.einsum("pcl,pdc->ld", draw_t, qkv_full, preferred_element_type=F32)
-    dn1 = lax.psum(dn1_part.astype(BF), "tensor").astype(F32)
+    draw_t = jnp.concatenate([dq_raw, dk_raw, dkv[heads_cols:]], axis=0).astype(BF)
+    dn1_part = jnp.einsum("cl,dc->ld", draw_t, qkv_full, preferred_element_type=F32)
+    dn1_low, ffn_total, g_ein, grad_eout, total_shared = lax.optimization_barrier(
+        (dn1_part.astype(BF), ffn_total, g_ein, grad_eout, total_shared)
+    )
+    layer_out = (resid + ffn_total.astype(F32)).astype(BF)
+    dn1 = lax.psum(dn1_low, "tensor")
     gain1_part = jnp.sum(dn1_part * n1, axis=0)
+    grad_qkv = jnp.einsum("ld,cl->dc", normed, draw_t, preferred_element_type=F32)
+    grad_outw = jnp.einsum("ld,cl->dc", dbranch, att_t, preferred_element_type=F32)
+    small = jnp.concatenate([router_part, gain1_part[:, None], gain2_part[:, None]], axis=1)
+    tail = own_sum(
+        jnp.concatenate([grad_qkv, grad_outw, small], axis=1), 0
+    )
+    total_qkv = tail[:, : 3 * heads_cols].reshape(-1, 3, heads_cols).transpose(1, 0, 2)
+    total_outw = tail[:, 3 * heads_cols : 4 * heads_cols]
+    small = lax.psum(tail[:, 4 * heads_cols :], "tensor")
+    g_ein = after(g_ein, tail)
+    if spread:
+        grad_ein = lax.all_to_all(g_ein, "ctx", split_axis=2, concat_axis=0, tiled=True)
+    else:
+        grad_ein = lax.psum_scatter(g_ein, "ctx", scatter_dimension=2, tiled=True)
+    dn1 = after(dn1, small, grad_ein).astype(F32)
     scaled1 = attn_gain * dn1
     grad_tokens = dresid + inv1 * (
         scaled1 - n1 * jnp.mean(scaled1 * n1, axis=-1, keepdims=True)
     )
-
-    grad_qkv = jnp.einsum("ld,pcl->dpc", normed, draw_t, preferred_element_type=F32)
-    grad_outw = jnp.einsum("ld,cl->dc", dbranch, att_t, preferred_element_type=F32)
-    small = jnp.concatenate([router_part, gain1_part[:, None], gain2_part[:, None]], axis=1)
-    tail = own_sum(
-        jnp.concatenate([grad_qkv.reshape(width, 3 * heads_cols), grad_outw, small], axis=1), 0
-    )
-    total_qkv = tail[:, : 3 * heads_cols].reshape(-1, 3, heads_cols).transpose(1, 0, 2)
-    total_outw = tail[:, 3 * heads_cols : 4 * heads_cols]
-    small = lax.psum(tail[:, 4 * heads_cols :], "tensor")
     return (
         layer_out[None],
         grad_tokens[None],
@@ -503,8 +534,8 @@
         total_outw,
         small[:, experts + 1],
         small[:, :experts],
-        total_shin,
-        total_shout,
+        total_shared[:2],
+        total_shared[2],
         grad_ein.astype(F32),
         grad_eout.astype(F32),
     )

time: 814 us -> 767 us (0.942)
  blocking collectives: 144 us -> 62.2 us
  waiting for transfers between devices: 284 us -> 338 us
  starting transfers between devices: 95.3 us -> 86.2 us
    all_gather x4 -> x0, blocking collectives: 102 us -> none  [the longest x1 52 us: shards(): shout_full = lax.all_gather(shared_out, DC, axis=0, tiled=True)]
    psum x3 -> x4, waiting for transfers between devices: 160 us -> 198 us  [the longest x1 88.1 us: shards(): branch = lax.psum(branch_part.astype(BF), 'tensor')]
    all_to_all x1, waiting for transfers between devices: 0.01 us -> 37 us  [shards(): lax.all_to_all(expert_in, 'ctx', split_axis=0, concat_axis=2, tiled=True)]
    ppermute x2, waiting for transfers between devices: 21.8 us -> 0.01 us  [shards(): dkv = dkv + lax.ppermute(piece.astype(BF), 'ctx', links).astype(F32)]
    all_to_all x1 -> x0, starting transfers between devices: 19.2 us -> none  [shards(): lax.all_to_all(expert_out, 'ctx', split_axis=0, concat_axis=1, tiled=True)]
    all_gather x1 -> x2, waiting for transfers between devices: 0.01 us -> 15.2 us  [the longest x1 15.1 us: shards(): thin_full = lax.all_gather(thin, DC, axis=0, tiled=True)]
    all_to_all x2, starting transfers between devices: 30.6 us -> 45 us  [own_sum(): lax.all_to_all(parts.astype(BF).reshape(cut), DC, split_axis=axis, concat...]
    all_to_all x1, blocking collectives: 16 us -> 28.3 us  [shards(): lax.all_to_all(expert_out, 'ctx', split_axis=0, concat_axis=1, tiled=True)]
  transfers between devices with their start and end apart: 19 -> 19, of which waited for: 9 -> 10; matrix products, arithmetic and copies ran while one was open for 18% -> 16% of each run, Pallas kernels for 7% -> 9%
where the time goes in v2:
time: 767 us; the launch traced here: 756 us
  waiting for transfers between devices  338 us (44%)
  starting transfers between devices  86.2 us (11%)
  Pallas kernels  69.8 us (9%)
  local copies, waits for them, and re-layouts  67.2 us (9%)
  matrix products  66.8 us (9%)
  blocking collectives  62.2 us (8%)
  other arithmetic  50.3 us (7%)
  between operations  15.1 us (2%)
    psum x1, waiting for transfers between devices, shards(): branch = lax.psum(branch_part.astype(BF), 'tensor')  88.1 us
    psum x1, waiting for transfers between devices, shards(): dn2 = lax.psum(dn2_low, 'tensor')  67.7 us
    all_to_all x4, waiting for transfers between devices, swap(): lax.all_to_all(values, expert_axes, split_axis=0, concat_axis=0, tiled=True)  65.2 us
    all_to_all x2, starting transfers between devices, own_sum(): lax.all_to_all(parts.astype(BF).reshape(cut), DC, split_axis=axis, concat...  45 us
    pallas_call x2, Pallas kernels, ffn(): pl.pallas_call(functools.partial(ffn_kernel, gated=gated), out_shape=outs...  41.9 us
    all_to_all x1, waiting for transfers between devices, shards(): lax.all_to_all(expert_in, 'ctx', split_axis=0, concat_axis=2, tiled=True)  37 us
    all_to_all x1, blocking collectives, shards(): lax.all_to_all(expert_out, 'ctx', split_axis=0, concat_axis=1, tiled=True)  28.3 us
    psum x1, waiting for transfers between devices, shards(): dn1 = lax.psum(dn1_low, 'tensor')  28.2 us
  transfers between devices with their start and end apart: 19, of which 10 were waited for; matrix products, arithmetic and copies ran while one was open for 16% of the time, Pallas kernels for 9%

profile of v2, /device:TPU:0, one launch (start us, length us, event | category | flops | bytes accessed | tf_op | source)
XLA Modules:
  0.0 756.0 jit_solution(16941534124955116927)
XLA Ops:
  24.1 15.1 %all-gather.3.cloned.1.call-done = bf16[768,786]{1,0:T(8,128)(2,1)} async-done(((bf16[96,786]{1,0:T(8,128)(2,1)}), bf16[768,786]{1,0:T(8,128)(2,1)}) %all-gather.3.cloned.1.call-update) | async-done | bytes 1207312 | tf_op jit(solution)/shard_map/all_gather | solution.py:333
  51.1 6.8 fusion.25
  57.8 11.1 %collective-permute-done = bf16[384,1024]{1,0:T(8,128)(2,1)S(1)} collective-permute-done((bf16[384,1024]{1,0:T(8,128)(2,1)S(1)}, bf16[384,1024]{1,0:T(8,128)(2,1)S(1)}, u32[]{:S(2)}, u32[]{:S(2)}) %collective-permute-start) | collective-permute-done | bytes 786464 | tf_op jit(solution)/shard_map/ppermute | solution.py:376
  70.5 28.3 %all_to_all.121 = bf16[8,192,512]{2,1,0:T(8,128)(2,1)S(1)} all-to-all(bf16[8,192,512]{2,1,0:T(8,128)(2,1)S(1)} %copy-done.14), channel_id=1, replica_groups=mesh['dp'=2,'ctx'=4,'tensor'=4] {'ctx'}, dimensions={0} | all-to-all | bytes 3145728 | tf_op jit(solution)/shard_map/all_to_all | solution.py:385
  98.8 4.6 all-to-all-start
  103.4 37.0 %all-to-all-done = bf16[8,2,192,512]{3,2,1,0:T(8,128)(2,1)} async-done(((bf16[8,2,192,512]{3,2,1,0:T(8,128)(2,1)}), bf16[8,2,192,512]{3,2,1,0:T(8,128)(2,1)}, u32[]{:S(2)}, u32[]{:S(2)}) %all-to-all-start) | async-done | bytes 3145760 | tf_op jit(solution)/shard_map/all_to_all | solution.py:384
  140.4 4.6 all-to-all-start.2
  150.9 13.0 %attn_fwd.1 = (bf16[192,1024]{1,0:T(8,128)(2,1)}, f32[3,1,1024]{2,1,0:T(1,128)}) custom-call(s32[4]{0:T(128)} %and_select_fusion.lo_ref, bf16[192,1024]{1,0:T(8,128)(2,1)} %bitcast.115, bf16[192,3072]{1,0:T(8,128)(2,1)} %get-tuple-element.168.k_ref, bf16[192,3072]{1,0:T(8,128)(2,1)} %get-tuple-element.167.v_ref, s32[1,1024]{1,0:T(1,128)} %bitcast.135), custom_call_target="tpu_custom_call" | custom-call | tf_op jit(solution)/shard_map/attn_fwd/pallas_call | solution.py:110
  172.1 88.1 %all-reduce.5.cloned.1.call-done = bf16[1024,768]{1,0:T(8,128)(2,1)} async-done(((bf16[1024,768]{1,0:T(8,128)(2,1)}), bf16[1024,768]{1,0:T(8,128)(2,1)}) %all-reduce.5.cloned.1.call-update) | async-done | bytes 1572880 | tf_op jit(solution)/shard_map/psum | solution.py:405
  262.9 6.8 fusion.28
  269.7 4.7 all-to-all-start.3
  278.6 41.1 %all-to-all-done.3.refs_0_ = bf16[8,2,160,768]{3,2,1,0:T(8,128)(2,1)} async-done(((bf16[8,2,160,768]{3,2,1,0:T(8,128)(2,1)}), bf16[8,2,160,768]{3,2,1,0:T(8,128)(2,1)}, u32[]{:S(2)}, u32[]{:S(2)}) %all-to-all-start.3) | async-done | bytes 3932192 | tf_op jit(solution)/shard_map/all_to_all | solution.py:349
  322.1 7.2 all_to_all.122
  331.6 28.5 %ffn_experts.1 = (bf16[8,2,160,768]{3,2,1,0:T(8,128)(2,1)}, bf16[8,2,160,768]{3,2,1,0:T(8,128)(2,1)}, f32[8,2,160,1]{3,2,1,0:T(8,128)}, bf16[2,2,768,512]{3,2,1,0:T(8,128)(2,1)}, bf16[2,768,512]{2,1,0:T(8,128)(2,1)}) custom-call(bf16[8,2,160,768]{3,2,1,0:T(8,128)(2,1)} %all-to-all-done.3.refs_0_, bf16[8,2,160,768]{3,2,1,0:T(8,128)(2,1)} %all-to-all-done.2.refs_1_, ...), custom_call_target="tpu_custom_call" | custom-call | tf_op jit(solution)/shard_map/ffn_experts/pallas_call | solution.py:232
  362.2 7.1 all_to_all.123
  369.2 4.7 all-to-all-start.5
  382.0 13.3 %ffn_shared.1 = (bf16[4,1,256,768]{3,2,1,0:T(8,128)(2,1)}, bf16[4,1,256,768]{3,2,1,0:T(8,128)(2,1)}, bf16[1,2,768,512]{3,2,1,0:T(8,128)(2,1)}, bf16[1,768,512]{2,1,0:T(8,128)(2,1)}) custom-call(bf16[4,1,256,768]{3,2,1,0:T(8,128)(2,1)} %bitcast.103, bf16[4,1,256,768]{3,2,1,0:T(8,128)(2,1)} %bitcast.107, bf16[1,2,768,512]{3,2,1,0:T(8,128)(2,1)} %slice_bitcast_fusion.refs_2_, ...), custom_call_target="tpu_custom_call" | custom-call | tf_op jit(solution)/shard_map/ffn_shared/pallas_call | solution.py:232
  395.3 24.0 %all-to-all-done.5 = bf16[8,2,160,768]{3,2,1,0:T(8,128)(2,1)} async-done(((bf16[8,2,160,768]{3,2,1,0:T(8,128)(2,1)}), bf16[8,2,160,768]{3,2,1,0:T(8,128)(2,1)}, u32[]{:S(2)}, u32[]{:S(2)}) %all-to-all-start.5) | async-done | bytes 3932192 | tf_op jit(solution)/shard_map/all_to_all | solution.py:349
  419.3 7.6 %fusion.5 = f32[1024,768]{1,0:T(8,128)S(1)} fusion(bf16[2560,768]{1,0:T(8,128)(2,1)} %bitcast.26, s32[1024]{0:T(1024)S(1)} %get-tuple-element.158, s32[1024]{0:T(1024)S(1)} %get-tuple-element.157), kind=kOutput, calls=%fused_computation.16 | convolution fusion | flops 4034396160 | bytes 7086080 | tf_op jit(solution)/shard_map/dot_general | solution.py:447
  430.7 4.5 all-to-all-start.7
  439.2 67.7 %all-reduce.7.cloned.1.call-done = bf16[1024,768]{1,0:T(8,128)(2,1)} async-done(((bf16[1024,768]{1,0:T(8,128)(2,1)}), bf16[1024,768]{1,0:T(8,128)(2,1)}) %all-reduce.7.cloned.1.call-update) | async-done | bytes 1572880 | tf_op jit(solution)/shard_map/psum | solution.py:464
  513.4 9.3 %fusion.43 = bf16[1024,768]{1,0:T(8,128)(2,1)} fusion(bf16[1024,768]{1,0:T(8,128)(2,1)S(1)} %bitcast.149, bf16[2560,768]{1,0:T(8,128)(2,1)} %bitcast.34, f32[1024]{0:T(1024)S(1)} %bitcast.146, s32[1024]{0:T(1024)S(1)} %get-tuple-element.158, f32[1024]{0:T(1024)S(1)} %bitcast.144, s32[1024]{0:T(1024)S(1)} %get-tuple-element.157), kind=kOutput, calls=%fused_computation.52 | convolution fusion | flops 4044619776 | bytes 7094272 | tf_op jit(solution)/shard_map/dot_general | solution.py:485
  533.7 15.0 %attn_bwd.1 = (f32[192,1024]{1,0:T(8,128)}, f32[192,3072]{1,0:T(8,128)}, f32[192,3072]{1,0:T(8,128)}) custom-call(s32[4]{0:T(128)} %and_select_fusion.lo_ref, bf16[192,1024]{1,0:T(8,128)(2,1)} %bitcast.116, bf16[192,3072]{1,0:T(8,128)(2,1)} %get-tuple-element.168.k_ref, bf16[192,3072]{1,0:T(8,128)(2,1)} %get-tuple-element.167.v_ref, ...), custom_call_target="tpu_custom_call" | custom-call | tf_op jit(solution)/shard_map/attn_bwd/pallas_call | solution.py:138
  559.0 31.2 %all-to-all-start.9 = ((bf16[3,8,96,512]{3,2,0,1:T(8,128)(2,1)}), bf16[3,8,96,512]{3,2,0,1:T(8,128)(2,1)}, u32[]{:S(2)}, u32[]{:S(2)}) async-start(bf16[3,8,96,512]{3,2,0,1:T(8,128)(2,1)} %copy.134), calls=%async_computation.9 | async-start | bytes 4718592 | tf_op jit(solution)/shard_map/all_to_all | solution.py:282
  618.2 11.5 %all-to-all-done.9 = bf16[3,8,96,512]{3,2,0,1:T(8,128)(2,1)} async-done(((bf16[3,8,96,512]{3,2,0,1:T(8,128)(2,1)}), bf16[3,8,96,512]{3,2,0,1:T(8,128)(2,1)}, u32[]{:S(2)}, u32[]{:S(2)}) %all-to-all-start.9) | async-done | bytes 2359328 | tf_op jit(solution)/shard_map/all_to_all | solution.py:282
  629.6 13.8 %all-to-all-start.10 = ((bf16[8,96,786]{2,1,0:T(8,128)(2,1)}), bf16[8,96,786]{2,1,0:T(8,128)(2,1)}, u32[]{:S(2)}, u32[]{:S(2)}) async-start(bf16[8,96,786]{2,1,0:T(8,128)(2,1)} %concatenate.50), calls=%async_computation.10 | async-start | bytes 2752512 | tf_op jit(solution)/shard_map/all_to_all | solution.py:282
  649.2 13.9 %all-reduce.9.cloned.1.call-done = bf16[1024,768]{1,0:T(8,128)(2,1)} async-done(((bf16[1024,768]{1,0:T(8,128)(2,1)}), bf16[1024,768]{1,0:T(8,128)(2,1)}) %all-reduce.9.cloned.1.call-update) | async-done | bytes 1572880 | tf_op jit(solution)/shard_map/psum | solution.py:489
  664.7 6.8 copy.140
  671.5 4.6 all-to-all-start.11
  679.6 19.6 %psum.39 = f32[96,18]{1,0:T(8,128)S(1)} all-reduce(f32[96,18]{1,0:T(8,128)S(1)} %slice.189), channel_id=1, replica_groups=mesh['dp'=2,'ctx'=4,'tensor'=4] {'tensor'}, use_global_device_ids=true, to_apply=%region_22.23 | all-reduce | flops 1728 | bytes 13824 | tf_op jit(solution)/shard_map/psum | solution.py:518
  707.5 28.2 %all-reduce.11.cloned.1.call-done = bf16[1024,768]{1,0:T(8,128)(2,1)} async-done(((bf16[1024,768]{1,0:T(8,128)(2,1)}), bf16[1024,768]{1,0:T(8,128)(2,1)}) %all-reduce.11.cloned.1.call-update) | async-done | bytes 1572880 | tf_op jit(solution)/shard_map/psum | solution.py:508
  738.2 4.4 fusion.41
  (193 shorter events, 156.8 us)
Async XLA Ops:
  7.2 32.0 %all-gather.3.cloned.1.call-start = ((), (), s32[]{:S(2)}) async-start(), calls=%async_computation.12 | async-start | bytes 1548288 | tf_op jit(solution)/shard_map/all_gather | solution.py:333
  12.5 9.1 %copy-start.6 = (s32[1,1024,2]{2,1,0:T(8,128)}, s32[1,1024,2]{2,1,0:T(8,128)S(1)}, u32[]{:S(2)}) copy-start(s32[1,1024,2]{2,1,0:T(8,128)S(1)} %copy.125) | copy-start | bytes 24580
  24.1 19.3 %copy-start.16 = (f32[32,1024]{1,0:T(8,128)}, f32[32,1024]{1,0:T(8,128)S(1)}, u32[]{:S(2)}) copy-start(f32[32,1024]{1,0:T(8,128)S(1)} %get-tuple-element.190) | copy-start | bytes 393220
  43.3 7.8 %copy-start.7 = (bf16[1,1024,768]{2,1,0:T(8,128)(2,1)S(1)}, bf16[1,1024,768]{2,1,0:T(8,128)(2,1)}, u32[]{:S(2)}) copy-start(bf16[1,1024,768]{2,1,0:T(8,128)(2,1)} %param.27) | copy-start | bytes 4718596
  45.1 12.8 %collective-permute-start.1 = (bf16[384,1024]{1,0:T(8,128)(2,1)S(1)}, bf16[384,1024]{1,0:T(8,128)(2,1)S(1)}, u32[]{:S(2)}, u32[]{:S(2)}) collective-permute-start(bf16[384,1024]{1,0:T(8,128)(2,1)S(1)} %pad_maximum_fusion.2), channel_id=1, source_target_pairs={{0,4},{4,8},{8,12},{1,5},{5,9},{9,13},{2,6},{6,10},{10,14},{3,7},{... | collective-permute-start | bytes 2359304 | tf_op jit(solution)/shard_map/ppermute | solution.py:376
  47.7 21.2 %collective-permute-start = (bf16[384,1024]{1,0:T(8,128)(2,1)S(1)}, bf16[384,1024]{1,0:T(8,128)(2,1)S(1)}, u32[]{:S(2)}, u32[]{:S(2)}) collective-permute-start(bf16[384,1024]{1,0:T(8,128)(2,1)S(1)} %pad_maximum_fusion.2), channel_id=1, source_target_pairs={{0,8},{4,12},{1,9},{5,13},{2,10},{6,14},{3,11},{7,15},{16,24},{20,... | collective-permute-start | bytes 2359304 | tf_op jit(solution)/shard_map/ppermute | solution.py:376
  57.8 12.7 %copy-start.14 = (bf16[8,192,512]{2,1,0:T(8,128)(2,1)S(1)}, bf16[8,192,512]{2,1,0:T(8,128)(2,1)}, u32[]{:S(2)}) copy-start(bf16[8,192,512]{2,1,0:T(8,128)(2,1)} %param.26) | copy-start | bytes 4718596
  98.8 41.6 %all-to-all-start = ((bf16[8,2,192,512]{3,2,1,0:T(8,128)(2,1)}), bf16[8,2,192,512]{3,2,1,0:T(8,128)(2,1)}, u32[]{:S(2)}, u32[]{:S(2)}) async-start(bf16[8,2,192,512]{3,2,1,0:T(8,128)(2,1)} %param.25), calls=%async_computation | async-start | bytes 6291456 | tf_op jit(solution)/shard_map/all_to_all | solution.py:384
  140.4 4.7 copy-start.28
  140.4 119.8 %all-to-all-start.2 = ((bf16[8,2,160,768]{3,2,1,0:T(8,128)(2,1)}), bf16[8,2,160,768]{3,2,1,0:T(8,128)(2,1)}, u32[]{:S(2)}, u32[]{:S(2)}) async-start(bf16[8,2,160,768]{3,2,1,0:T(8,128)(2,1)} %bitcast.111), calls=%async_computation.2 | async-start | bytes 7864320 | tf_op jit(solution)/shard_map/all_to_all | solution.py:349
  145.0 115.2 %all-reduce.5.cloned.1.call-start = ((), (), s32[]{:S(2)}) async-start(), calls=%async_computation.13 | async-start | bytes 3145728 | tf_op jit(solution)/shard_map/psum | solution.py:405
  145.4 5.6 copy-start.27
  262.9 6.8 copy-start.3
  269.7 6.1 copy-start.25
  269.7 6.1 copy-start.26
  269.7 50.0 %all-to-all-start.3 = ((bf16[8,2,160,768]{3,2,1,0:T(8,128)(2,1)}), bf16[8,2,160,768]{3,2,1,0:T(8,128)(2,1)}, u32[]{:S(2)}, u32[]{:S(2)}) async-start(bf16[8,2,160,768]{3,2,1,0:T(8,128)(2,1)} %bitcast.112), calls=%async_computation.3 | async-start | bytes 7864320 | tf_op jit(solution)/shard_map/all_to_all | solution.py:349
  274.4 102.9 %all-gather.5.cloned.1.call-start = ((), (), s32[]{:S(2)}) async-start(), calls=%async_computation.14 | async-start | bytes 2654208 | tf_op jit(solution)/shard_map/all_gather | solution.py:426
  369.2 50.1 %all-to-all-start.5 = ((bf16[8,2,160,768]{3,2,1,0:T(8,128)(2,1)}), bf16[8,2,160,768]{3,2,1,0:T(8,128)(2,1)}, u32[]{:S(2)}, u32[]{:S(2)}) async-start(bf16[8,2,160,768]{3,2,1,0:T(8,128)(2,1)} %get-tuple-element.57), calls=%async_computation.5 | async-start | bytes 7864320 | tf_op jit(solution)/shard_map/all_to_all | solution.py:349
  377.2 49.7 %copy-start.24 = (bf16[1024,16]{0,1:T(8,128)(2,1)}, bf16[1024,16]{0,1:T(8,128)(2,1)S(1)}, u32[]{:S(2)}) copy-start(bf16[1024,16]{0,1:T(8,128)(2,1)S(1)} %select_reduce_fusion.2) | copy-start | bytes 98308
  419.3 7.6 %copy-start.13 = (bf16[4,1,256,768]{3,2,1,0:T(8,128)(2,1)S(1)}, bf16[4,1,256,768]{3,2,1,0:T(8,128)(2,1)}, u32[]{:S(2)}) copy-start(bf16[4,1,256,768]{3,2,1,0:T(8,128)(2,1)} %get-tuple-element.61) | copy-start | bytes 4718596
  430.7 76.1 %all-to-all-start.7 = ((bf16[8,2,160,768]{3,2,1,0:T(8,128)(2,1)}), bf16[8,2,160,768]{3,2,1,0:T(8,128)(2,1)}, u32[]{:S(2)}, u32[]{:S(2)}) async-start(bf16[8,2,160,768]{3,2,1,0:T(8,128)(2,1)} %get-tuple-element.64), calls=%async_computation.7 | async-start | bytes 7864320 | tf_op jit(solution)/shard_map/all_to_all | solution.py:349
  435.3 71.6 %all-reduce.7.cloned.1.call-start = ((), (), s32[]{:S(2)}) async-start(), calls=%async_computation.15 | async-start | bytes 3145728 | tf_op jit(solution)/shard_map/psum | solution.py:464
  529.4 29.6 %all-to-all-start.8 = ((bf16[2,768,512]{2,0,1:T(2,128)(2,1)}), bf16[2,768,512]{2,0,1:T(2,128)(2,1)}, u32[]{:S(2)}, u32[]{:S(2)}) async-start(bf16[2,768,512]{2,0,1:T(2,128)(2,1)} %copy.132), calls=%async_computation.8 | async-start | bytes 3145728 | tf_op jit(solution)/shard_map/all_to_all | solution.py:470
  554.7 44.7 %collective-permute-start.3 = (bf16[384,1024]{1,0:T(8,128)(2,1)}, bf16[384,1024]{1,0:T(8,128)(2,1)}, u32[]{:S(2)}, u32[]{:S(2)}) collective-permute-start(bf16[384,1024]{1,0:T(8,128)(2,1)} %get-tuple-element.166), channel_id=1, source_target_pairs={{8,0},{12,4},{9,1},{13,5},{10,2},{14,6},{11,3},{15,7},{24,16},{28,... | collective-permute-start | bytes 2359304 | tf_op jit(solution)/shard_map/ppermute | solution.py:499
  556.1 43.3 %collective-permute-start.2 = (bf16[384,1024]{1,0:T(8,128)(2,1)}, bf16[384,1024]{1,0:T(8,128)(2,1)}, u32[]{:S(2)}, u32[]{:S(2)}) collective-permute-start(bf16[384,1024]{1,0:T(8,128)(2,1)} %get-tuple-element.165), channel_id=1, source_target_pairs={{4,0},{8,4},{12,8},{5,1},{9,5},{13,9},{6,2},{10,6},{14,10},{7,3},{... | collective-permute-start | bytes 2359304 | tf_op jit(solution)/shard_map/ppermute | solution.py:499
  559.0 35.2 %copy-start.10 = (bf16[192,1024]{1,0:T(8,128)(2,1)S(1)}, bf16[192,1024]{1,0:T(8,128)(2,1)}, u32[]{:S(2)}) copy-start(bf16[192,1024]{1,0:T(8,128)(2,1)} %get-tuple-element.49.o_ref) | copy-start | bytes 1179652
  559.0 70.7 %all-to-all-start.9 = ((bf16[3,8,96,512]{3,2,0,1:T(8,128)(2,1)}), bf16[3,8,96,512]{3,2,0,1:T(8,128)(2,1)}, u32[]{:S(2)}, u32[]{:S(2)}) async-start(bf16[3,8,96,512]{3,2,0,1:T(8,128)(2,1)} %copy.134), calls=%async_computation.9 | async-start | bytes 4718592 | tf_op jit(solution)/shard_map/all_to_all | solution.py:282
  590.1 73.0 %all-reduce.9.cloned.1.call-start = ((), (), s32[]{:S(2)}) async-start(), calls=%async_computation.16 | async-start | bytes 3145728 | tf_op jit(solution)/shard_map/psum | solution.py:489
  601.8 4.8 copy-start.21
  629.6 33.5 %all-to-all-start.10 = ((bf16[8,96,786]{2,1,0:T(8,128)(2,1)}), bf16[8,96,786]{2,1,0:T(8,128)(2,1)}, u32[]{:S(2)}, u32[]{:S(2)}) async-start(bf16[8,96,786]{2,1,0:T(8,128)(2,1)} %concatenate.50), calls=%async_computation.10 | async-start | bytes 2752512 | tf_op jit(solution)/shard_map/all_to_all | solution.py:282
  643.4 92.3 %all-reduce.11.cloned.1.call-start = ((), (), s32[]{:S(2)}) async-start(), calls=%async_computation.17 | async-start | bytes 3145728 | tf_op jit(solution)/shard_map/psum | solution.py:508
  671.5 71.0 %all-to-all-start.11 = ((bf16[2,2,768,512]{3,1,0,2:T(2,128)(2,1)}), bf16[2,2,768,512]{3,1,0,2:T(2,128)(2,1)}, u32[]{:S(2)}, u32[]{:S(2)}) async-start(bf16[2,2,768,512]{3,1,0,2:T(2,128)(2,1)} %copy.140), calls=%async_computation.11 | async-start | bytes 6291456 | tf_op jit(solution)/shard_map/all_to_all | solution.py:521
  (18 other events, 51.5 us)
Sparse Core Ops, SparseCore 0:
  11.7 27.5 all-gather.2
  167.2 92.9 all-reduce.4
  319.9 27.1 all-gather.4
  438.1 68.6 all-reduce.6
  594.2 68.8 all-reduce.8
  665.9 69.7 all-reduce.10
